TPU v7x, 512 devices: a whole 4x8x8 slice. The times are simulated.
512 devices in a mesh: row: 16 (over y, x_hi), col: 16 (over z, core), rep: 2 (over x_lo).
Axes of the slice: x: 4 (x_hi: 2, x_lo: 2; x = x_hi * 2 + x_lo), y: 8, z: 8, core: 2. Of those that a mesh axis runs over, the one named last changes fastest.
Arguments:
- amplitudes: bfloat16 [64, 64, 6, 5184], P('row', 'col', 'rep'), may hold values from -6 to 6
- integrals: bfloat16 [5184, 6, 5184], P('col', 'rep', 'row'), may hold values from -0.03125 to 0.03125
- occ_offsets: int32 [9], replicated, may hold values from 0 to 64, as said below
- slab: int32 [2], replicated, may hold values from 0 to 7
Outputs:
- residual: bfloat16 [64, 64, 5184], P('row', 'col')
Inputs may be any that keep to these rules, and one draw needn't show every extreme that they name: `occ_offsets`: never falling; entry 0 is 0 and entry 8 is 64; entries k and k+1 bound the occupied orbitals of irrep k.
All inputs are finite; a program needn't handle non-finite values.
Results may differ from a plain program's by a relative error of at most 0.02.
Values may be sent and summed in bfloat16 or wider, within the bound.
No kernel may reach another device: no remote copies, remote signals or barrier semaphores. Data moves between devices by JAX's collectives and lax.ppermute only.
A program may use at most 128 MiB of HBM per device.

v0:
```python
import jax
import jax.numpy as jnp
from jax import lax
from jax.sharding import PartitionSpec as P


def irrep_labels(orbitals, occ_offsets):
    return jnp.sum((orbitals[:, None] >= occ_offsets[None, 1:8]).astype(jnp.int32), axis=1)


def shards(amplitudes, integrals, occ_offsets, slab):
    block_rows = amplitudes.shape[0]
    shuffled = lax.all_to_all(amplitudes, "row", split_axis=3, concat_axis=0, tiled=True)
    slab_rows = lax.all_gather(integrals, "col", axis=0, tiled=True)
    summed = lax.psum_scatter(
        jnp.einsum("ijkc,akc->ija", shuffled, slab_rows, preferred_element_type=jnp.float32).astype(
            jnp.bfloat16
        ),
        "row",
        scatter_dimension=0,
        tiled=True,
    )
    ladder = lax.psum(summed, "rep")
    sectioned = lax.all_to_all(
        lax.all_to_all(ladder[None], "row", split_axis=3, concat_axis=0, tiled=True),
        "col",
        split_axis=0,
        concat_axis=0,
        tiled=True,
    )
    mirrored = lax.all_to_all(sectioned, "row", split_axis=0, concat_axis=3, tiled=True)
    mirror = jnp.swapaxes(mirrored[0], 0, 1)
    local_range = jnp.arange(block_rows, dtype=jnp.int32)
    row_orbitals = lax.axis_index("row") * block_rows + local_range
    col_orbitals = lax.axis_index("col") * block_rows + local_range
    target = jnp.bitwise_xor(slab[0], slab[1])
    row_labels = irrep_labels(row_orbitals, occ_offsets)
    col_labels = irrep_labels(col_orbitals, occ_offsets)
    allowed = jnp.bitwise_xor(row_labels[:, None], col_labels[None, :]) == target
    mixed = ladder.astype(jnp.float32) - mirror.astype(jnp.float32)
    return jnp.where(allowed[:, :, None], mixed, jnp.float32(0.0)).astype(jnp.bfloat16)


def solution(mesh):
    placed = (P("row", "col", "rep", None), P("col", "rep", "row"), P(), P())
    return jax.shard_map(
        shards, mesh=mesh, in_specs=placed, out_specs=P("row", "col", None), check_vma=False
    )
```

profile of v0, /device:TPU:1, one launch (start us, length us, event | category | flops | bytes accessed | tf_op | source)
XLA Modules:
  0.0 432.6 jit_solution(2016425769477299145)
XLA Ops:
  6.5 0.0 all-gather.2.cloned.1.call-start
  6.5 2.5 copy.26
  9.0 0.0 all-gather.2.cloned.1.call-update
  9.1 0.0 all-reduce.6.cloned.1.call-start
  9.1 18.9 %copy.24 = bf16[4,4,3,5184]{1,0,2,3:T(4,128)(2,1)} copy(bf16[4,4,3,5184]{3,1,2,0:T(4,128)(2,1)} %param.4) | data formatting | bytes 995328 | tf_op args[0]
  28.0 19.7 %reshape.50 = bf16[16,2,7776]{2,1,0:T(2,128)(2,1)S(1)} reshape(bf16[5184,3,4,4]{3,2,1,0:T(4,128)(2,1)} %bitcast.42) | data formatting | bytes 995328
  47.7 27.0 %all_to_all.50 = bf16[16,2,7776]{2,1,0:T(2,128)(2,1)S(1)} all-to-all(bf16[16,2,7776]{2,1,0:T(2,128)(2,1)S(1)} %reshape.50), channel_id=1, replica_groups=mesh['row'=16,'col'=16,'rep'=2] {'row'}, dimensions={0} | all-to-all | bytes 995328 | tf_op jit(solution)/shard_map/all_to_all | solution.py:13
  74.7 20.0 %reshape.51 = bf16[5184,3,4,4]{3,2,1,0:T(4,128)(2,1)} reshape(bf16[16,2,7776]{2,1,0:T(2,128)(2,1)S(1)} %all_to_all.50) | data formatting | bytes 995328
  94.7 18.4 %copy.25 = bf16[4,4,3,16,324]{4,0,3,2,1:T(4,128)(2,1)S(1)} copy(bf16[4,4,3,16,324]{1,0,2,4,3:T(4,128)(2,1)} %bitcast.41) | data formatting | bytes 995328 | tf_op jit(solution)/shard_map/all_to_all | solution.py:13
  113.2 0.3 all_to_all.39
  113.5 0.0 all-gather.2.cloned.1.call-done
  113.5 10.8 %fusion.6 = bf16[64,4,5184]{2,0,1:T(8,128)(2,1)} fusion(bf16[64,4,3,324]{3,0,2,1:T(8,128)(2,1)S(1)} %all_to_all.39, bf16[5184,3,324]{2,1,0:T(4,128)(2,1)} %all-gather.2.cloned.1.call-done), kind=kOutput, calls=%fused_computation.4 | convolution fusion | flops 2581217280 | bytes 13229568 | tf_op jit(solution)/shard_map/ijkc,akc->ija/dot_general | solution.py:16
  124.3 0.0 all-reduce.6.cloned.1.call-update
  124.3 0.0 copy-start.2
  124.3 0.0 copy-start.1
  124.3 0.0 all-reduce.4.cloned.1.call-start
  124.4 1.3 dynamic-slice
  126.3 168.0 %all-reduce.6.cloned.1.call-done = bf16[64,4,5184]{2,0,1:T(8,128)(2,1)} async-done(((bf16[64,4,5184]{2,0,1:T(8,128)(2,1)}), bf16[64,4,5184]{2,0,1:T(8,128)(2,1)}) %all-reduce.6.cloned.1.call-update) | async-done | bytes 2654224
  294.3 1.7 constant_dynamic-slice_fusion
  296.1 0.0 all-reduce.4.cloned.1.call-update
  296.1 47.9 %all-reduce.4.cloned.1.call-done = bf16[4,4,5184]{2,0,1:T(4,128)(2,1)} async-done(((bf16[4,4,5184]{2,0,1:T(4,128)(2,1)}), bf16[4,4,5184]{2,0,1:T(4,128)(2,1)}) %all-reduce.4.cloned.1.call-update) | async-done | bytes 165904 | tf_op jit(solution)/shard_map/psum | solution.py:23
  344.0 0.0 copy-start
  344.0 6.8 %copy.28 = bf16[1,4,4,5184]{1,2,0,3:T(4,128)(2,1)} copy(bf16[1,4,4,5184]{3,1,2,0:T(4,128)(2,1)} %bitcast.46) | data formatting | bytes 331776 | tf_op jit(solution)/shard_map/broadcast_in_dim | solution.py:25
  350.8 6.4 %reshape.52 = bf16[16,2,2592]{2,1,0:T(2,128)(2,1)S(1)} reshape(bf16[5184,1,4,4]{3,2,1,0:T(4,128)(2,1)} %bitcast.43) | data formatting | bytes 331776
  357.3 18.8 %all_to_all.51 = bf16[16,2,2592]{2,1,0:T(2,128)(2,1)S(1)} all-to-all(bf16[16,2,2592]{2,1,0:T(2,128)(2,1)S(1)} %reshape.52), channel_id=1, replica_groups=mesh['row'=16,'col'=16,'rep'=2] {'row'}, dimensions={0} | all-to-all | bytes 331776 | tf_op jit(solution)/shard_map/all_to_all | solution.py:25
  376.1 5.7 %reshape.53 = bf16[5184,1,4,4]{3,2,1,0:T(4,128)(2,1)} reshape(bf16[16,2,2592]{2,1,0:T(2,128)(2,1)S(1)} %all_to_all.51) | data formatting | bytes 331776
  381.8 7.2 %copy.29 = bf16[1,4,4,16,324]{4,1,2,3,0:T(4,128)(2,1)} copy(bf16[1,4,4,16,324]{1,2,4,3,0:T(4,128)(2,1)} %bitcast.44) | data formatting | bytes 331776 | tf_op jit(solution)/shard_map/all_to_all | solution.py:25
  388.9 9.9 %all-to-all-start.2 = ((bf16[16,4,4,324]{3,1,2,0:T(4,128)(2,1)}), bf16[16,4,4,324]{3,1,2,0:T(4,128)(2,1)}, u32[]{:S(2)}, u32[]{:S(2)}) async-start(bf16[16,4,4,324]{3,1,2,0:T(4,128)(2,1)} %bitcast.9), calls=%async_computation.2 | async-start | bytes 393216 | tf_op jit(solution)/shard_map/all_to_all | solution.py:24
  398.9 0.0 copy-done.2
  398.9 0.1 slice.10
  399.0 0.0 copy-done.1
  399.0 0.6 fusion.11
  400.9 8.3 %all-to-all-done.2 = bf16[16,4,4,324]{3,1,2,0:T(4,128)(2,1)} async-done(((bf16[16,4,4,324]{3,1,2,0:T(4,128)(2,1)}), bf16[16,4,4,324]{3,1,2,0:T(4,128)(2,1)}, u32[]{:S(2)}, u32[]{:S(2)}) %all-to-all-start.2) | async-done | bytes 165920 | tf_op jit(solution)/shard_map/all_to_all | solution.py:24
  409.2 3.5 all-to-all-start.3
  412.7 0.2 convert_reduce_fusion.1
  412.9 0.1 xor_compare_fusion
  413.0 11.6 %all-to-all-done.3 = bf16[16,4,4,324]{3,1,2,0:T(4,128)(2,1)S(1)} async-done(((bf16[16,4,4,324]{3,1,2,0:T(4,128)(2,1)}), bf16[16,4,4,324]{3,1,2,0:T(4,128)(2,1)S(1)}, u32[]{:S(2)}, u32[]{:S(2)}) %all-to-all-start.3) | async-done | bytes 165920 | tf_op jit(solution)/shard_map/all_to_all | solution.py:31
  424.7 0.1 copy.30
  424.8 0.4 reshape.43
  425.2 0.0 copy-done
  425.2 0.1 fusion.10
  425.4 0.7 copy.31
  (2 shorter events, 0.0 us)
Async XLA Ops:
  6.5 106.9 %all-gather.2.cloned.1.call-start = ((), (), s32[]{:S(2)}) async-start(), calls=%async_computation.4 | async-start | bytes 16920576 | tf_op jit(solution)/shard_map/all_gather | solution.py:14
  9.1 285.3 %all-reduce.6.cloned.1.call-start = ((), (), s32[]{:S(2)}) async-start(), calls=%async_computation.6 | async-start | bytes 5373952
  124.3 274.6 %copy-start.2 = (s32[9]{0:T(128)S(1)}, s32[9]{0:T(128)}, u32[]{:S(2)}) copy-start(s32[9]{0:T(128)} %param.6) | copy-start | bytes 112
  124.3 274.7 %copy-start.1 = (s32[2]{0:T(128)S(1)}, s32[2]{0:T(128)}, u32[]{:S(2)}) copy-start(s32[2]{0:T(128)} %param.7) | copy-start | bytes 28
  124.3 219.7 %all-reduce.4.cloned.1.call-start = ((), (), s32[]{:S(2)}) async-start(), calls=%async_computation.5 | async-start | bytes 335872 | tf_op jit(solution)/shard_map/psum | solution.py:23
  344.0 81.2 %copy-start = (bf16[4,4,5184]{2,0,1:T(4,128)(2,1)S(1)}, bf16[4,4,5184]{2,0,1:T(4,128)(2,1)}, u32[]{:S(2)}) copy-start(bf16[4,4,5184]{2,0,1:T(4,128)(2,1)} %all-reduce.4.cloned.1.call-done) | copy-start | bytes 497668
  388.9 20.3 %all-to-all-start.2 = ((bf16[16,4,4,324]{3,1,2,0:T(4,128)(2,1)}), bf16[16,4,4,324]{3,1,2,0:T(4,128)(2,1)}, u32[]{:S(2)}, u32[]{:S(2)}) async-start(bf16[16,4,4,324]{3,1,2,0:T(4,128)(2,1)} %bitcast.9), calls=%async_computation.2 | async-start | bytes 393216 | tf_op jit(solution)/shard_map/all_to_all | solution.py:24
  409.2 15.5 %all-to-all-start.3 = ((bf16[16,4,4,324]{3,1,2,0:T(4,128)(2,1)}), bf16[16,4,4,324]{3,1,2,0:T(4,128)(2,1)S(1)}, u32[]{:S(2)}, u32[]{:S(2)}) async-start(bf16[16,4,4,324]{3,1,2,0:T(4,128)(2,1)} %all-to-all-done.2), calls=%async_computation.3 | async-start | bytes 393216 | tf_op jit(solution)/shard_map/all_to_all | solution.py:31
Sparse Core Ops, SparseCore 0:
  9.5 100.6 all-gather.1
  124.4 169.8 all-reduce.5
  297.2 46.7 all-reduce.3
where the time goes:
time: 436 us; the launch traced here: 433 us
  waiting for transfers between devices  236 us (54%)
  local copies, waits for them, and re-layouts  111 us (25%)
  blocking collectives  45.8 us (11%)
  between operations  15.2 us (3%)
  starting transfers between devices  13.6 us (3%)
  matrix products  10.8 us (2%)
    unnamed x4, waiting for transfers between devices  168 us
    unnamed x14, local copies, waits for them, and re-layouts  76.2 us
    psum x1, waiting for transfers between devices, shards(): ladder = lax.psum(summed, 'rep')  47.9 us
    all_to_all x1, blocking collectives, shards(): lax.all_to_all(amplitudes, 'row', split_axis=3, concat_axis=0, tiled=True)  27 us
    all_to_all x1, blocking collectives, shards(): lax.all_to_all(ladder[None], 'row', split_axis=3, concat_axis=0, tiled=True)  18.8 us
    all_to_all x2, local copies, waits for them, and re-layouts, shards(): lax.all_to_all(amplitudes, 'row', split_axis=3, concat_axis=0, tiled=True)  18.7 us
    all_to_all x1, waiting for transfers between devices, shards(): lax.all_to_all(sectioned, 'row', split_axis=0, concat_axis=3, tiled=True)  11.6 us
    dot_general x1, matrix products, shards(): jnp.einsum('ijkc,akc->ija', shuffled, slab_rows, preferred_element_type=j...  10.8 us
  transfers between devices with their start and end apart: 5, of which 4 were waited for; matrix products, arithmetic and copies ran while one was open for 18% of the time, Pallas kernels for 0%

commit v1 on v0

v1 whole, which is shorter than its diff:
```python
import functools

import jax
import jax.numpy as jnp
import numpy as np
from jax import lax
from jax.experimental import pallas as pl
from jax.experimental.pallas import tpu as pltpu
from jax.sharding import Mesh, PartitionSpec as P

BF = jnp.bfloat16
F32 = jnp.float32
AXES = ("y", "xh", "z", "core", "xl")
PLANE = ("y", "xh", "xl")
ROW = ("y", "xh")
TARGET = ("y", "xh", "core")
VM = pl.BlockSpec(memory_space=pltpu.VMEM)
SM = pl.BlockSpec(memory_space=pltpu.SMEM)


def cost(flops, nbytes):
    return pl.CostEstimate(flops=flops, bytes_accessed=nbytes, transcendentals=0)


def pack_a_kernel(rows, sub, a_ref, o_ref):
    ni, nk, nj, _ = a_ref.shape
    for r in range(rows):
        for i in range(ni):
            piece = jnp.concatenate([a_ref[i, k, :, r * sub : (r + 1) * sub] for k in range(nk)], axis=1)
            for p in range(o_ref.shape[1]):
                o_ref[r, p, i * nj : (i + 1) * nj, :] = piece


def pack_b_kernel(p_ref, b_ref, keep_ref, send_ref):
    full = jnp.concatenate([b_ref[k] for k in range(b_ref.shape[0])], axis=1)
    half = full.shape[0] // 2
    pad = jnp.zeros((keep_ref.shape[0] - half, full.shape[1]), full.dtype)
    low = jnp.concatenate([full[:half], pad], axis=0)
    high = jnp.concatenate([full[half:], pad], axis=0)
    first = p_ref[0] == 0

    @pl.when(first)
    def _():
        keep_ref[...] = low
        send_ref[...] = high

    @pl.when(jnp.logical_not(first))
    def _():
        keep_ref[...] = high
        send_ref[...] = low


def join_kernel(x_ref, y_ref, o_ref):
    o_ref[0] = x_ref[...]
    o_ref[1] = y_ref[...]


def contract_kernel(half, form, pos_ref, own_ref, oth_ref, *refs):
    o_ref = refs[-1]
    halves, at = [], 0
    for count in form:
        if count == 1:
            halves.append((refs[at][0], refs[at][1]))
        else:
            halves.append((refs[at][...], refs[at + 1][...]))
        at += count
    core, p = pos_ref[0], pos_ref[1]
    dims = (((1,), (1,)), ((), ()))
    rt, _, mi, kc = own_ref.shape
    for slot, ref in ((core, own_ref), (1 - core, oth_ref)):
        lhs = [ref[:, pl.ds(h, 1)].reshape(rt * mi, kc) for h in (p, 1 - p)]
        parts = []
        for rhs in halves:
            acc = lax.dot_general(lhs[0], rhs[0], dims, preferred_element_type=F32)
            acc += lax.dot_general(lhs[1], rhs[1], dims, preferred_element_type=F32)
            parts.append(acc[:, :half])
        full = parts[0] if len(parts) == 1 else jnp.concatenate(parts, axis=1)
        o_ref[:, pl.ds(slot, 1), :, :] = full.astype(BF).reshape(rt, 1, mi, full.shape[1])


def take_half_kernel(x_ref, o_ref):
    o_ref[...] = x_ref[0]


def take_half(x, p):
    _, half, kc = x.shape
    return pl.pallas_call(
        take_half_kernel,
        grid=(1,),
        in_specs=[pl.BlockSpec((1, half, kc), lambda s: (p, 0, 0))],
        out_specs=pl.BlockSpec((half, kc), lambda s: (0, 0)),
        out_shape=jax.ShapeDtypeStruct((half, kc), x.dtype),
        cost_estimate=cost(0, 4 * half * kc),
        compiler_params=pltpu.CompilerParams(vmem_limit_bytes=4 << 20),
    )(x)


def contract(pos, own, oth, blocks, half):
    rt, _, mi, kc = own.shape
    width = half * len(blocks)
    refs = [r for block in blocks for r in block]
    return pl.pallas_call(
        functools.partial(contract_kernel, half, tuple(len(block) for block in blocks)),
        in_specs=[SM] + [VM] * (2 + len(refs)),
        out_specs=VM,
        out_shape=jax.ShapeDtypeStruct((rt, 2, mi, width), BF),
        cost_estimate=cost(2 * 2 * rt * mi * 2 * kc * width, 2 * (4 * rt * mi * kc + width * 2 * kc + 2 * rt * mi * width)),
        compiler_params=pltpu.CompilerParams(vmem_limit_bytes=24 << 20),
    )(pos, own, oth, *refs)


def gather_sum_kernel(layout, half, z_ref, *refs):
    chunks, o_ref = refs[:-1], refs[-1]
    nz = o_ref.shape[0]
    for x_ref, offs in zip(chunks, layout):
        for core in range(x_ref.shape[1]):
            total = x_ref[0, core].astype(F32)
            for s in range(1, x_ref.shape[0]):
                total += x_ref[s, core].astype(F32)
            total = total.astype(BF)
            for b, off in enumerate(offs):
                at = lax.rem(z_ref[0] + off + nz, nz)
                o_ref[pl.ds(at, 1), core] = total[:, b * half : (b + 1) * half][None]


def antisym_kernel(pos_ref, occ_ref, slab_ref, s_ref, m_ref, o_ref):
    target = slab_ref[0] ^ slab_ref[1]
    n = s_ref.shape[2]
    side = 4
    r = lax.broadcasted_iota(jnp.int32, (n, 1), 0)
    ri = lax.broadcasted_iota(jnp.int32, (n, n), 0)
    ci = lax.broadcasted_iota(jnp.int32, (n, n), 1)
    swap = jnp.where((ri // side == ci % side) & (ri % side == ci // side), 1.0, 0.0).astype(BF)
    i_orb = pos_ref[0] * side + r // side
    j_orb = pos_ref[1] * side + r % side
    i_lab = jnp.zeros((n, 1), jnp.int32)
    j_lab = jnp.zeros((n, 1), jnp.int32)
    for k in range(1, 8):
        i_lab += (i_orb >= occ_ref[k]).astype(jnp.int32)
        j_lab += (j_orb >= occ_ref[k]).astype(jnp.int32)
    allowed = (i_lab ^ j_lab) == target
    for z in range(s_ref.shape[0]):
        for core in range(s_ref.shape[1]):
            flipped = jnp.dot(swap, m_ref[z, core], preferred_element_type=F32)
            mixed = s_ref[z, core].astype(F32) - flipped
            o_ref[z, core] = jnp.where(allowed, mixed, 0.0).astype(BF)


def assemble_kernel(p_ref, own_ref, oth_ref, o_ref):
    first = p_ref[0] == 0
    nj = o_ref.shape[1]

    def write(low_ref, high_ref):
        for i in range(o_ref.shape[0]):
            rows = slice(i * nj, (i + 1) * nj)
            parts = [
                ref[z, core, rows, :]
                for z in range(own_ref.shape[0])
                for core in range(own_ref.shape[1])
                for ref in (low_ref, high_ref)
            ]
            o_ref[i] = jnp.concatenate(parts, axis=1)

    @pl.when(first)
    def _():
        write(own_ref, oth_ref)

    @pl.when(jnp.logical_not(first))
    def _():
        write(oth_ref, own_ref)


def kernel_call(body, outs, in_specs, args, nbytes):
    many = isinstance(outs, (list, tuple))
    return pl.pallas_call(
        body,
        in_specs=in_specs,
        out_specs=[VM] * len(outs) if many else VM,
        out_shape=outs,
        cost_estimate=cost(nbytes, nbytes),
        compiler_params=pltpu.CompilerParams(vmem_limit_bytes=12 << 20),
    )(*args)


def residual_of(amplitudes, integrals, occ_offsets, slab):
    ni, nj, nk, nc = amplitudes.shape
    na, _, sub = integrals.shape
    rows = nc // sub
    half = na // 2
    kc = nk * sub

    def at(*axes):
        place = 0
        for axis in axes:
            place = place * lax.axis_size(axis) + lax.axis_index(axis)
        return place.astype(jnp.int32)

    def shift(x, axis, by):
        n = lax.axis_size(axis)
        return lax.ppermute(x, axis, [(d, (d + by) % n) for d in range(n)])

    mine = at("xl").reshape(1)
    padded = -(-half // 8) * 8
    keep, send = kernel_call(
        pack_b_kernel,
        [jax.ShapeDtypeStruct((padded, kc), BF)] * 2,
        [SM, VM],
        (mine, jnp.transpose(integrals, (1, 0, 2))),
        4 * na * kc,
    )
    packed_a = kernel_call(
        functools.partial(pack_a_kernel, rows, sub),
        jax.ShapeDtypeStruct((rows, 2, ni * nj, kc), BF),
        [VM],
        (jnp.transpose(amplitudes, (0, 2, 1, 3)),),
        6 * ni * nj * nk * nc,
    )
    recv = shift(send, "xl", 1)

    ring = {}
    for way, by in (("up", 1), ("down", -1)):
        first = shift(keep, "z", by)
        second = shift(recv, "z", by)
        ring[way, 1] = kernel_call(
            join_kernel,
            jax.ShapeDtypeStruct((2, padded, kc), BF),
            [VM, VM],
            (first, second),
            8 * padded * kc,
        )
        for t in (2, 3):
            ring[way, t] = shift(ring[way, t - 1], "z", by)
    far = []
    for p, (way, by) in enumerate((("up", 1), ("down", -1))):
        part = take_half(ring[way, 3], p)
        far.append(shift(part, "z", by))

    own = lax.all_to_all(
        packed_a.reshape(rows * 2, ni * nj, kc), PLANE, split_axis=0, concat_axis=0, tiled=True
    ).reshape(rows, 2, ni * nj, kc)
    oth = shift(own, "core", 1)

    plan = (
        ((0, -1, 1, -2, 2), [(keep, recv)] + [(ring[way, t],) for t in (1, 2) for way in ("up", "down")]),
        ((-3, 3, 4), [(ring["up", 3],), (ring["down", 3],), tuple(far)]),
    )
    layout = [offs for offs, _ in plan]
    pos = jnp.stack([at("core"), at("xl")])
    pieces = []
    for _, blocks in plan:
        part = contract(pos, own, oth, blocks, half)
        _, _, n, width = part.shape
        part = part.reshape(rows * 2, n, width)
        part = lax.all_to_all(part, TARGET, split_axis=0, concat_axis=0, tiled=True)
        pieces.append(part.reshape(rows, 2, n, width))

    n = ni * nj
    held = jax.ShapeDtypeStruct((lax.axis_size("z"), 2, n, half), BF)
    nbytes = 2 * lax.axis_size("z") * 2 * n * half
    total = kernel_call(
        functools.partial(gather_sum_kernel, layout, half),
        held,
        [SM] + [VM] * len(pieces),
        (at("z").reshape(1), *pieces),
        rows * nbytes,
    )

    shape = tuple(lax.axis_size(a) for a in AXES)
    pairs = []
    for at_y, at_xh, at_z, at_core, at_xl in np.ndindex(*shape):
        here, there = (at_y, at_xh, at_z, at_core, at_xl), (at_z, at_core, at_y, at_xh, at_xl)
        pairs.append((int(np.ravel_multi_index(here, shape)), int(np.ravel_multi_index(there, shape))))
    mirrored = lax.ppermute(total, AXES, pairs)
    mixed = kernel_call(
        antisym_kernel,
        held,
        [SM, SM, SM, VM, VM],
        (jnp.stack([at(*ROW), at("z", "core")]), occ_offsets, slab, total, mirrored),
        3 * nbytes,
    )
    other = shift(mixed, "xl", 1)
    return kernel_call(
        assemble_kernel,
        jax.ShapeDtypeStruct((ni, nj, lax.axis_size("z") * 4 * half), BF),
        [SM, VM, VM],
        (mine, mixed, other),
        4 * nbytes,
    )


def solution(mesh):
    fine = Mesh(mesh.devices.reshape(8, 2, 8, 2, 2), AXES)
    row, col = ROW, ("z", "core")
    placed = (P(row, col, "xl", None), P(col, "xl", row), P(), P())
    return jax.shard_map(
        residual_of, mesh=fine, in_specs=placed, out_specs=P(row, col, None), check_vma=False
    )
```

time: 436 us -> 201 us (0.46)
  the two profiles are of different devices: /device:TPU:1 before, /device:TPU:57 now
where the time goes in v1:
time: 201 us; the launch traced here: 200 us
  starting transfers between devices  96.3 us (48%)
  waiting for transfers between devices  81.9 us (41%)
  Pallas kernels  14.8 us (7%)
  local copies, waits for them, and re-layouts  6.83 us (3%)
    ppermute x13, starting transfers between devices, shift(): return lax.ppermute(x, axis, [(d, (d + by) % n) for d in range(n)])  51.7 us
    ppermute x13, waiting for transfers between devices, shift(): return lax.ppermute(x, axis, [(d, (d + by) % n) for d in range(n)])  39.4 us
    all_to_all x2, waiting for transfers between devices, residual_of(): part = lax.all_to_all(part, TARGET, split_axis=0, concat_axis=0, tiled=True)  31.4 us
    all_to_all x2, starting transfers between devices, residual_of(): part = lax.all_to_all(part, TARGET, split_axis=0, concat_axis=0, tiled=True)  24.8 us
    ppermute x1, waiting for transfers between devices, residual_of(): mirrored = lax.ppermute(total, AXES, pairs)  11.1 us
    ppermute x1, starting transfers between devices, residual_of(): mirrored = lax.ppermute(total, AXES, pairs)  10.7 us
    all_to_all x1, starting transfers between devices, residual_of(): lax.all_to_all(packed_a.reshape(rows * 2, ni * nj, kc), PLANE, split_axis...  9.12 us
    pallas_call x2, Pallas kernels, contract(): pl.pallas_call(functools.partial(contract_kernel, half, tuple((len(block)...  8.15 us
  transfers between devices with their start and end apart: 17, of which 11 were waited for; matrix products, arithmetic and copies ran while one was open for 0% of the time, Pallas kernels for 4%

profile of v1, /device:TPU:57, one launch (start us, length us, event | category | flops | bytes accessed | tf_op | source)
XLA Modules:
  0.0 200.3 jit_solution(11387987209233502980)
XLA Ops:
  0.0 0.0 copy-start.6
  0.0 1.0 copy-done.6
  1.0 1.7 shard_map.46
  2.8 9.1 %all-to-all-start = ((bf16[32,16,972]{2,1,0:T(8,128)(2,1)}), bf16[32,16,972]{2,1,0:T(8,128)(2,1)S(1)}, u32[]{:S(2)}, u32[]{:S(2)}) async-start(bf16[32,16,972]{2,1,0:T(8,128)(2,1)} %bitcast.6), calls=%async_computation | async-start | bytes 2097152 | tf_op jit(solution)/shard_map/all_to_all | solution.py:238
  11.9 0.0 copy-done.5
  11.9 0.2 shard_map.47
  12.2 0.0 copy-start.7
  12.2 3.1 %collective-permute-start.1 = (bf16[168,972]{1,0:T(8,128)(2,1)S(1)}, bf16[168,972]{1,0:T(8,128)(2,1)S(1)}, u32[]{:S(2)}, u32[]{:S(2)}) collective-permute-start(bf16[168,972]{1,0:T(8,128)(2,1)S(1)} %get-tuple-element.8), channel_id=1, source_target_pairs={{0,1},{1,0},{2,3},{3,2},{4,5},{5,4},{6,7},{7,6},{8,9},{9,8},{10,11... | collective-permute-start | bytes 979784 | tf_op jit(solution)/shard_map/ppermute | solution.py:200
  15.3 4.0 %collective-permute-start.2 = (bf16[168,972]{1,0:T(8,128)(2,1)S(1)}, bf16[168,972]{1,0:T(8,128)(2,1)S(1)}, u32[]{:S(2)}, u32[]{:S(2)}) collective-permute-start(bf16[168,972]{1,0:T(8,128)(2,1)S(1)} %get-tuple-element.7.refs_0_), channel_id=1, source_target_pairs={{0,4},{4,8},{8,12},{12,16},{16,20},{20,24},{24,28},{28,0},{1,5},{5... | collective-permute-start | bytes 979784 | tf_op jit(solution)/shard_map/ppermute | solution.py:200
  19.3 10.4 %collective-permute-done.1.refs_1_ = bf16[168,972]{1,0:T(8,128)(2,1)S(1)} collective-permute-done((bf16[168,972]{1,0:T(8,128)(2,1)S(1)}, bf16[168,972]{1,0:T(8,128)(2,1)S(1)}, u32[]{:S(2)}, u32[]{:S(2)}) %collective-permute-start.1) | collective-permute-done | bytes 326624 | tf_op jit(solution)/shard_map/ppermute | solution.py:200
  29.7 4.0 %collective-permute-start.3 = (bf16[168,972]{1,0:T(8,128)(2,1)S(1)}, bf16[168,972]{1,0:T(8,128)(2,1)S(1)}, u32[]{:S(2)}, u32[]{:S(2)}) collective-permute-start(bf16[168,972]{1,0:T(8,128)(2,1)S(1)} %collective-permute-done.1.refs_1_), channel_id=1, source_target_pairs={{0,4},{4,8},{8,12},{12,16},{16,20},{20,24},{24,28},{28,0},{1,5},{5... | collective-permute-start | bytes 979784 | tf_op jit(solution)/shard_map/ppermute | solution.py:200
  33.7 8.6 %collective-permute-start.4 = (bf16[168,972]{1,0:T(8,128)(2,1)S(1)}, bf16[168,972]{1,0:T(8,128)(2,1)S(1)}, u32[]{:S(2)}, u32[]{:S(2)}) collective-permute-start(bf16[168,972]{1,0:T(8,128)(2,1)S(1)} %get-tuple-element.7.refs_0_), channel_id=1, source_target_pairs={{0,28},{4,0},{8,4},{12,8},{16,12},{20,16},{24,20},{28,24},{1,29},{... | collective-permute-start | bytes 979784 | tf_op jit(solution)/shard_map/ppermute | solution.py:200
  42.3 3.4 %collective-permute-start.5 = (bf16[168,972]{1,0:T(8,128)(2,1)S(1)}, bf16[168,972]{1,0:T(8,128)(2,1)S(1)}, u32[]{:S(2)}, u32[]{:S(2)}) collective-permute-start(bf16[168,972]{1,0:T(8,128)(2,1)S(1)} %collective-permute-done.1.refs_1_), channel_id=1, source_target_pairs={{0,28},{4,0},{8,4},{12,8},{16,12},{20,16},{24,20},{28,24},{1,29},{... | collective-permute-start | bytes 979784 | tf_op jit(solution)/shard_map/ppermute | solution.py:200
  45.7 0.0 collective-permute-done.2.x_ref
  45.7 1.1 collective-permute-done.3.y_ref
  46.8 0.0 copy-done.7
  46.8 0.0 copy-done.9
  46.8 1.9 collective-permute-start.6
  48.8 0.0 collective-permute-done.4.x_ref
  48.8 6.3 %collective-permute-done.5.y_ref = bf16[168,972]{1,0:T(8,128)(2,1)S(1)} collective-permute-done((bf16[168,972]{1,0:T(8,128)(2,1)S(1)}, bf16[168,972]{1,0:T(8,128)(2,1)S(1)}, u32[]{:S(2)}, u32[]{:S(2)}) %collective-permute-start.5) | collective-permute-done | bytes 326624 | tf_op jit(solution)/shard_map/ppermute | solution.py:200
  55.1 5.3 %collective-permute-start.7 = (bf16[2,168,972]{2,1,0:T(8,128)(2,1)S(1)}, bf16[2,168,972]{2,1,0:T(8,128)(2,1)}, u32[]{:S(2)}, u32[]{:S(2)}) collective-permute-start(bf16[2,168,972]{2,1,0:T(8,128)(2,1)S(1)} %shard_map.49.refs_3_), channel_id=1, source_target_pairs={{0,28},{4,0},{8,4},{12,8},{16,12},{20,16},{24,20},{28,24},{1,29},{... | collective-permute-start | bytes 1959560 | tf_op jit(solution)/shard_map/ppermute | solution.py:200
  60.4 0.0 all-to-all-done
  60.4 5.1 %collective-permute-start = (bf16[16,2,16,972]{3,2,1,0:T(8,128)(2,1)S(1)}, bf16[16,2,16,972]{3,2,1,0:T(8,128)(2,1)S(1)}, u32[]{:S(2)}, u32[]{:S(2)}) collective-permute-start(bf16[16,2,16,972]{3,2,1,0:T(8,128)(2,1)S(1)} %bitcast.13), channel_id=1, source_target_pairs={{0,2},{2,0},{1,3},{3,1},{4,6},{6,4},{5,7},{7,5},{8,10},{10,8},{9,1... | collective-permute-start | bytes 2985992 | tf_op jit(solution)/shard_map/ppermute | solution.py:200
  65.5 0.0 collective-permute-done.6.refs_4_
  65.6 1.9 collective-permute-start.8
  67.5 4.8 %collective-permute-done.7.refs_5_ = bf16[2,168,972]{2,1,0:T(8,128)(2,1)} collective-permute-done((bf16[2,168,972]{2,1,0:T(8,128)(2,1)S(1)}, bf16[2,168,972]{2,1,0:T(8,128)(2,1)}, u32[]{:S(2)}, u32[]{:S(2)}) %collective-permute-start.7) | collective-permute-done | bytes 653216 | tf_op jit(solution)/shard_map/ppermute | solution.py:200
  72.3 5.4 %collective-permute-start.9 = (bf16[2,168,972]{2,1,0:T(8,128)(2,1)}, bf16[2,168,972]{2,1,0:T(8,128)(2,1)S(1)}, u32[]{:S(2)}, u32[]{:S(2)}) collective-permute-start(bf16[2,168,972]{2,1,0:T(8,128)(2,1)} %collective-permute-done.7.refs_5_), channel_id=1, source_target_pairs={{0,28},{4,0},{8,4},{12,8},{16,12},{20,16},{24,20},{28,24},{1,29},{... | collective-permute-start | bytes 1959560 | tf_op jit(solution)/shard_map/ppermute | solution.py:200
  77.7 5.8 %collective-permute-done.8.x_ref.refs_0_ = bf16[2,168,972]{2,1,0:T(8,128)(2,1)S(1)} collective-permute-done((bf16[2,168,972]{2,1,0:T(8,128)(2,1)}, bf16[2,168,972]{2,1,0:T(8,128)(2,1)S(1)}, u32[]{:S(2)}, u32[]{:S(2)}) %collective-permute-start.8) | collective-permute-done | bytes 653216 | tf_op jit(solution)/shard_map/ppermute | solution.py:200
  83.5 0.8 shard_map.51
  84.3 1.9 collective-permute-start.10
  86.2 2.8 %collective-permute-done.9.x_ref.refs_1_ = bf16[2,168,972]{2,1,0:T(8,128)(2,1)S(1)} collective-permute-done((bf16[2,168,972]{2,1,0:T(8,128)(2,1)}, bf16[2,168,972]{2,1,0:T(8,128)(2,1)S(1)}, u32[]{:S(2)}, u32[]{:S(2)}) %collective-permute-start.9) | collective-permute-done | bytes 653216 | tf_op jit(solution)/shard_map/ppermute | solution.py:200
  89.1 0.7 shard_map.52
  89.8 0.0 copy-done
  89.8 0.8 copy-done.2
  90.7 5.2 %collective-permute-start.11 = (bf16[168,972]{1,0:T(8,128)(2,1)}, bf16[168,972]{1,0:T(8,128)(2,1)}, u32[]{:S(2)}, u32[]{:S(2)}) collective-permute-start(bf16[168,972]{1,0:T(8,128)(2,1)} %shard_map.52), channel_id=1, source_target_pairs={{0,28},{4,0},{8,4},{12,8},{16,12},{20,16},{24,20},{28,24},{1,29},{... | collective-permute-start | bytes 979784 | tf_op jit(solution)/shard_map/ppermute | solution.py:200
  95.9 0.1 pad_add_fusion.1.pos_ref
  95.9 0.0 collective-permute-done.10.refs_2_
  96.0 4.4 %collective-permute-done.11.refs_3_ = bf16[168,972]{1,0:T(8,128)(2,1)} collective-permute-done((bf16[168,972]{1,0:T(8,128)(2,1)}, bf16[168,972]{1,0:T(8,128)(2,1)}, u32[]{:S(2)}, u32[]{:S(2)}) %collective-permute-start.11) | collective-permute-done | bytes 326624 | tf_op jit(solution)/shard_map/ppermute | solution.py:200
  100.4 0.0 collective-permute-done.oth_ref
  100.4 1.1 copy-done.1
  101.5 1.1 copy-done.3
  102.6 3.0 %shard_map.53 = bf16[16,2,16,486]{3,2,1,0:T(8,128)(2,1)S(1)} custom-call(s32[2]{0:T(128)S(1)} %pad_add_fusion.1.pos_ref, bf16[16,2,16,972]{3,2,1,0:T(8,128)(2,1)S(1)} %bitcast.14, bf16[16,2,16,972]{3,2,1,0:T(8,128)(2,1)S(1)} %collective-permute-done.oth_ref, bf16[2,168,972]{2,1,0:T(8,128)(2,1)S(1)} %copy-done.1, bf16[2,168,972]{2,1,0:T(8,128)(2,1)S(1)} %copy-done.3, ...), custom_call_target="tpu_custom_call" | custom-call | flops 967458816 | bytes 4377888 | tf_op jit(solution)/shard_map/pallas_call | solution.py:102
  105.5 0.0 copy-start.4
  105.5 0.8 copy-done.4
  106.3 17.3 %all-to-all-start.2 = ((bf16[32,16,486]{2,1,0:T(8,128)(2,1)}), bf16[32,16,486]{2,1,0:T(8,128)(2,1)}, u32[]{:S(2)}, u32[]{:S(2)}) async-start(bf16[32,16,486]{2,1,0:T(8,128)(2,1)} %bitcast.17), calls=%async_computation.2 | async-start | bytes 1048576 | tf_op jit(solution)/shard_map/all_to_all | solution.py:254
  123.6 0.0 copy-start.8
  123.6 1.0 copy-done.8
  124.6 1.0 copy-done.10
  125.6 5.2 %shard_map.50 = bf16[16,2,16,810]{3,2,1,0:T(8,128)(2,1)} custom-call(s32[2]{0:T(128)S(1)} %pad_add_fusion.1.pos_ref, bf16[16,2,16,972]{3,2,1,0:T(8,128)(2,1)S(1)} %bitcast.15, bf16[16,2,16,972]{3,2,1,0:T(8,128)(2,1)S(1)} %collective-permute-done.oth_ref, bf16[168,972]{1,0:T(8,128)(2,1)S(1)} %copy-done.8, bf16[168,972]{1,0:T(8,128)(2,1)S(1)} %copy-done.10, ...), custom_call_target="tpu_custom_call" | custom-call | flops 1612431360 | bytes 5969376 | tf_op jit(solution)/shard_map/pallas_call | solution.py:102
  130.8 8.1 %all-to-all-done.2 = bf16[32,16,486]{2,1,0:T(8,128)(2,1)} async-done(((bf16[32,16,486]{2,1,0:T(8,128)(2,1)}), bf16[32,16,486]{2,1,0:T(8,128)(2,1)}, u32[]{:S(2)}, u32[]{:S(2)}) %all-to-all-start.2) | async-done | bytes 497696 | tf_op jit(solution)/shard_map/all_to_all | solution.py:254
  138.8 7.5 %all-to-all-start.1 = ((bf16[32,16,810]{2,1,0:T(8,128)(2,1)}), bf16[32,16,810]{2,1,0:T(8,128)(2,1)S(1)}, u32[]{:S(2)}, u32[]{:S(2)}) async-start(bf16[32,16,810]{2,1,0:T(8,128)(2,1)} %bitcast.9), calls=%async_computation.1 | async-start | bytes 1835008 | tf_op jit(solution)/shard_map/all_to_all | solution.py:254
  146.4 23.3 %all-to-all-done.1 = bf16[32,16,810]{2,1,0:T(8,128)(2,1)S(1)} async-done(((bf16[32,16,810]{2,1,0:T(8,128)(2,1)}), bf16[32,16,810]{2,1,0:T(8,128)(2,1)S(1)}, u32[]{:S(2)}, u32[]{:S(2)}) %all-to-all-start.1) | async-done | bytes 829472 | tf_op jit(solution)/shard_map/all_to_all | solution.py:254
  169.7 1.3 shard_map.54.s_ref
  171.0 10.7 %collective-permute-start.12 = (bf16[8,2,16,162]{3,2,1,0:T(8,128)(2,1)S(1)}, bf16[8,2,16,162]{3,2,1,0:T(8,128)(2,1)S(1)}, u32[]{:S(2)}, u32[]{:S(2)}) collective-permute-start(bf16[8,2,16,162]{3,2,1,0:T(8,128)(2,1)S(1)} %shard_map.54.s_ref), channel_id=1, source_target_pairs={{0,0},{1,1},{2,32},{3,33},{4,64},{5,65},{6,96},{7,97},{8,128},{9,1... | collective-permute-start | bytes 248840 | tf_op jit(solution)/shard_map/ppermute | solution.py:273
  181.7 0.0 copy-start.11
  181.7 0.0 copy-start.12
  181.7 0.1 pad_add_fusion.pos_ref
  181.8 11.1 %collective-permute-done.12.m_ref = bf16[8,2,16,162]{3,2,1,0:T(8,128)(2,1)S(1)} collective-permute-done((bf16[8,2,16,162]{3,2,1,0:T(8,128)(2,1)S(1)}, bf16[8,2,16,162]{3,2,1,0:T(8,128)(2,1)S(1)}, u32[]{:S(2)}, u32[]{:S(2)}) %collective-permute-start.12) | collective-permute-done | bytes 82976 | tf_op jit(solution)/shard_map/ppermute | solution.py:273
  192.9 0.0 copy-done.11
  192.9 0.0 copy-done.12
  192.9 0.7 shard_map.55.own_ref
  193.6 1.9 collective-permute-start.13
  195.5 3.8 %collective-permute-done.13.oth_ref = bf16[8,2,16,162]{3,2,1,0:T(8,128)(2,1)S(1)} collective-permute-done((bf16[8,2,16,162]{3,2,1,0:T(8,128)(2,1)S(1)}, bf16[8,2,16,162]{3,2,1,0:T(8,128)(2,1)S(1)}, u32[]{:S(2)}, u32[]{:S(2)}) %collective-permute-start.13) | collective-permute-done | bytes 82976 | tf_op jit(solution)/shard_map/ppermute | solution.py:200
  199.3 1.0 shard_map.56
  (9 shorter events, 0.1 us)
Async XLA Ops:
  0.0 1.0 copy-start.6
  2.8 9.1 %copy-start.5 = (bf16[324,3,324]{2,0,1:T(8,128)(2,1)S(1)}, bf16[324,3,324]{2,0,1:T(8,128)(2,1)}, u32[]{:S(2)}) copy-start(bf16[324,3,324]{2,0,1:T(8,128)(2,1)} %param.5) | copy-start | bytes 1889572
  2.8 57.7 %all-to-all-start = ((bf16[32,16,972]{2,1,0:T(8,128)(2,1)}), bf16[32,16,972]{2,1,0:T(8,128)(2,1)S(1)}, u32[]{:S(2)}, u32[]{:S(2)}) async-start(bf16[32,16,972]{2,1,0:T(8,128)(2,1)} %bitcast.6), calls=%async_computation | async-start | bytes 2097152 | tf_op jit(solution)/shard_map/all_to_all | solution.py:238
  12.2 34.7 %copy-start.7 = (bf16[168,972]{1,0:T(8,128)(2,1)}, bf16[168,972]{1,0:T(8,128)(2,1)S(1)}, u32[]{:S(2)}) copy-start(bf16[168,972]{1,0:T(8,128)(2,1)S(1)} %get-tuple-element.7.refs_0_) | copy-start | bytes 979780
  12.2 17.6 %collective-permute-start.1 = (bf16[168,972]{1,0:T(8,128)(2,1)S(1)}, bf16[168,972]{1,0:T(8,128)(2,1)S(1)}, u32[]{:S(2)}, u32[]{:S(2)}) collective-permute-start(bf16[168,972]{1,0:T(8,128)(2,1)S(1)} %get-tuple-element.8), channel_id=1, source_target_pairs={{0,1},{1,0},{2,3},{3,2},{4,5},{5,4},{6,7},{7,6},{8,9},{9,8},{10,11... | collective-permute-start | bytes 979784 | tf_op jit(solution)/shard_map/ppermute | solution.py:200
  15.3 30.4 %collective-permute-start.2 = (bf16[168,972]{1,0:T(8,128)(2,1)S(1)}, bf16[168,972]{1,0:T(8,128)(2,1)S(1)}, u32[]{:S(2)}, u32[]{:S(2)}) collective-permute-start(bf16[168,972]{1,0:T(8,128)(2,1)S(1)} %get-tuple-element.7.refs_0_), channel_id=1, source_target_pairs={{0,4},{4,8},{8,12},{12,16},{16,20},{20,24},{24,28},{28,0},{1,5},{5... | collective-permute-start | bytes 979784 | tf_op jit(solution)/shard_map/ppermute | solution.py:200
  29.7 17.1 %copy-start.9 = (bf16[168,972]{1,0:T(8,128)(2,1)}, bf16[168,972]{1,0:T(8,128)(2,1)S(1)}, u32[]{:S(2)}) copy-start(bf16[168,972]{1,0:T(8,128)(2,1)S(1)} %collective-permute-done.1.refs_1_) | copy-start | bytes 979780
  29.7 17.0 %collective-permute-start.3 = (bf16[168,972]{1,0:T(8,128)(2,1)S(1)}, bf16[168,972]{1,0:T(8,128)(2,1)S(1)}, u32[]{:S(2)}, u32[]{:S(2)}) collective-permute-start(bf16[168,972]{1,0:T(8,128)(2,1)S(1)} %collective-permute-done.1.refs_1_), channel_id=1, source_target_pairs={{0,4},{4,8},{8,12},{12,16},{16,20},{20,24},{24,28},{28,0},{1,5},{5... | collective-permute-start | bytes 979784 | tf_op jit(solution)/shard_map/ppermute | solution.py:200
  33.7 15.0 %collective-permute-start.4 = (bf16[168,972]{1,0:T(8,128)(2,1)S(1)}, bf16[168,972]{1,0:T(8,128)(2,1)S(1)}, u32[]{:S(2)}, u32[]{:S(2)}) collective-permute-start(bf16[168,972]{1,0:T(8,128)(2,1)S(1)} %get-tuple-element.7.refs_0_), channel_id=1, source_target_pairs={{0,28},{4,0},{8,4},{12,8},{16,12},{20,16},{24,20},{28,24},{1,29},{... | collective-permute-start | bytes 979784 | tf_op jit(solution)/shard_map/ppermute | solution.py:200
  42.3 12.7 %collective-permute-start.5 = (bf16[168,972]{1,0:T(8,128)(2,1)S(1)}, bf16[168,972]{1,0:T(8,128)(2,1)S(1)}, u32[]{:S(2)}, u32[]{:S(2)}) collective-permute-start(bf16[168,972]{1,0:T(8,128)(2,1)S(1)} %collective-permute-done.1.refs_1_), channel_id=1, source_target_pairs={{0,28},{4,0},{8,4},{12,8},{16,12},{20,16},{24,20},{28,24},{1,29},{... | collective-permute-start | bytes 979784 | tf_op jit(solution)/shard_map/ppermute | solution.py:200
  46.8 18.7 %collective-permute-start.6 = (bf16[2,168,972]{2,1,0:T(8,128)(2,1)S(1)}, bf16[2,168,972]{2,1,0:T(8,128)(2,1)}, u32[]{:S(2)}, u32[]{:S(2)}) collective-permute-start(bf16[2,168,972]{2,1,0:T(8,128)(2,1)S(1)} %shard_map.48.refs_2_), channel_id=1, source_target_pairs={{0,4},{4,8},{8,12},{12,16},{16,20},{20,24},{24,28},{28,0},{1,5},{5... | collective-permute-start | bytes 1959560 | tf_op jit(solution)/shard_map/ppermute | solution.py:200
  55.1 17.2 %collective-permute-start.7 = (bf16[2,168,972]{2,1,0:T(8,128)(2,1)S(1)}, bf16[2,168,972]{2,1,0:T(8,128)(2,1)}, u32[]{:S(2)}, u32[]{:S(2)}) collective-permute-start(bf16[2,168,972]{2,1,0:T(8,128)(2,1)S(1)} %shard_map.49.refs_3_), channel_id=1, source_target_pairs={{0,28},{4,0},{8,4},{12,8},{16,12},{20,16},{24,20},{28,24},{1,29},{... | collective-permute-start | bytes 1959560 | tf_op jit(solution)/shard_map/ppermute | solution.py:200
  60.4 39.9 %collective-permute-start = (bf16[16,2,16,972]{3,2,1,0:T(8,128)(2,1)S(1)}, bf16[16,2,16,972]{3,2,1,0:T(8,128)(2,1)S(1)}, u32[]{:S(2)}, u32[]{:S(2)}) collective-permute-start(bf16[16,2,16,972]{3,2,1,0:T(8,128)(2,1)S(1)} %bitcast.13), channel_id=1, source_target_pairs={{0,2},{2,0},{1,3},{3,1},{4,6},{6,4},{5,7},{7,5},{8,10},{10,8},{9,1... | collective-permute-start | bytes 2985992 | tf_op jit(solution)/shard_map/ppermute | solution.py:200
  65.6 18.0 %collective-permute-start.8 = (bf16[2,168,972]{2,1,0:T(8,128)(2,1)}, bf16[2,168,972]{2,1,0:T(8,128)(2,1)S(1)}, u32[]{:S(2)}, u32[]{:S(2)}) collective-permute-start(bf16[2,168,972]{2,1,0:T(8,128)(2,1)} %collective-permute-done.6.refs_4_), channel_id=1, source_target_pairs={{0,4},{4,8},{8,12},{12,16},{16,20},{20,24},{24,28},{28,0},{1,5},{5... | collective-permute-start | bytes 1959560 | tf_op jit(solution)/shard_map/ppermute | solution.py:200
  72.3 16.7 %collective-permute-start.9 = (bf16[2,168,972]{2,1,0:T(8,128)(2,1)}, bf16[2,168,972]{2,1,0:T(8,128)(2,1)S(1)}, u32[]{:S(2)}, u32[]{:S(2)}) collective-permute-start(bf16[2,168,972]{2,1,0:T(8,128)(2,1)} %collective-permute-done.7.refs_5_), channel_id=1, source_target_pairs={{0,28},{4,0},{8,4},{12,8},{16,12},{20,16},{24,20},{28,24},{1,29},{... | collective-permute-start | bytes 1959560 | tf_op jit(solution)/shard_map/ppermute | solution.py:200
  83.5 6.3 %copy-start = (bf16[2,168,972]{2,1,0:T(8,128)(2,1)}, bf16[2,168,972]{2,1,0:T(8,128)(2,1)S(1)}, u32[]{:S(2)}) copy-start(bf16[2,168,972]{2,1,0:T(8,128)(2,1)S(1)} %collective-permute-done.8.x_ref.refs_0_) | copy-start | bytes 1959556
  84.3 11.6 %collective-permute-start.10 = (bf16[168,972]{1,0:T(8,128)(2,1)}, bf16[168,972]{1,0:T(8,128)(2,1)}, u32[]{:S(2)}, u32[]{:S(2)}) collective-permute-start(bf16[168,972]{1,0:T(8,128)(2,1)} %shard_map.51), channel_id=1, source_target_pairs={{0,4},{4,8},{8,12},{12,16},{16,20},{20,24},{24,28},{28,0},{1,5},{5... | collective-permute-start | bytes 979784 | tf_op jit(solution)/shard_map/ppermute | solution.py:200
  89.8 0.8 copy-start.2
  90.7 9.7 %collective-permute-start.11 = (bf16[168,972]{1,0:T(8,128)(2,1)}, bf16[168,972]{1,0:T(8,128)(2,1)}, u32[]{:S(2)}, u32[]{:S(2)}) collective-permute-start(bf16[168,972]{1,0:T(8,128)(2,1)} %shard_map.52), channel_id=1, source_target_pairs={{0,28},{4,0},{8,4},{12,8},{16,12},{20,16},{24,20},{28,24},{1,29},{... | collective-permute-start | bytes 979784 | tf_op jit(solution)/shard_map/ppermute | solution.py:200
  100.4 1.1 copy-start.1
  101.5 1.1 copy-start.3
  105.5 0.8 copy-start.4
  106.3 32.5 %all-to-all-start.2 = ((bf16[32,16,486]{2,1,0:T(8,128)(2,1)}), bf16[32,16,486]{2,1,0:T(8,128)(2,1)}, u32[]{:S(2)}, u32[]{:S(2)}) async-start(bf16[32,16,486]{2,1,0:T(8,128)(2,1)} %bitcast.17), calls=%async_computation.2 | async-start | bytes 1048576 | tf_op jit(solution)/shard_map/all_to_all | solution.py:254
  123.6 1.0 copy-start.8
  124.6 1.0 copy-start.10
  138.8 30.9 %all-to-all-start.1 = ((bf16[32,16,810]{2,1,0:T(8,128)(2,1)}), bf16[32,16,810]{2,1,0:T(8,128)(2,1)S(1)}, u32[]{:S(2)}, u32[]{:S(2)}) async-start(bf16[32,16,810]{2,1,0:T(8,128)(2,1)} %bitcast.9), calls=%async_computation.1 | async-start | bytes 1835008 | tf_op jit(solution)/shard_map/all_to_all | solution.py:254
  171.0 21.9 %collective-permute-start.12 = (bf16[8,2,16,162]{3,2,1,0:T(8,128)(2,1)S(1)}, bf16[8,2,16,162]{3,2,1,0:T(8,128)(2,1)S(1)}, u32[]{:S(2)}, u32[]{:S(2)}) collective-permute-start(bf16[8,2,16,162]{3,2,1,0:T(8,128)(2,1)S(1)} %shard_map.54.s_ref), channel_id=1, source_target_pairs={{0,0},{1,1},{2,32},{3,33},{4,64},{5,65},{6,96},{7,97},{8,128},{9,1... | collective-permute-start | bytes 248840 | tf_op jit(solution)/shard_map/ppermute | solution.py:273
  181.7 11.2 %copy-start.11 = (s32[9]{0:T(128)S(1)}, s32[9]{0:T(128)}, u32[]{:S(2)}) copy-start(s32[9]{0:T(128)} %occ_ref.1) | copy-start | bytes 112
  181.7 11.2 %copy-start.12 = (s32[2]{0:T(128)S(1)}, s32[2]{0:T(128)}, u32[]{:S(2)}) copy-start(s32[2]{0:T(128)} %slab_ref.1) | copy-start | bytes 28
  193.6 5.7 %collective-permute-start.13 = (bf16[8,2,16,162]{3,2,1,0:T(8,128)(2,1)S(1)}, bf16[8,2,16,162]{3,2,1,0:T(8,128)(2,1)S(1)}, u32[]{:S(2)}, u32[]{:S(2)}) collective-permute-start(bf16[8,2,16,162]{3,2,1,0:T(8,128)(2,1)S(1)} %shard_map.55.own_ref), channel_id=1, source_target_pairs={{0,1},{1,0},{2,3},{3,2},{4,5},{5,4},{6,7},{7,6},{8,9},{9,8},{10,11... | collective-permute-start | bytes 248840 | tf_op jit(solution)/shard_map/ppermute | solution.py:200

commit v2 on v0

v2 whole, which is shorter than its diff:
```python
import functools

import jax
import jax.numpy as jnp
import numpy as np
from jax import lax
from jax.experimental import pallas as pl
from jax.experimental.pallas import tpu as pltpu
from jax.sharding import Mesh, PartitionSpec as P

BF = jnp.bfloat16
F32 = jnp.float32
AXES = ("y", "xh", "z", "core", "xl")
ROW = ("xh", "y")
TARGET = ("xh", "y", "core")
VM = pl.BlockSpec(memory_space=pltpu.VMEM)
SM = pl.BlockSpec(memory_space=pltpu.SMEM)


def cost(flops, nbytes):
    return pl.CostEstimate(flops=flops, bytes_accessed=nbytes, transcendentals=0)


def pack_a_kernel(rows, sub, a_ref, o_ref):
    ni, nk, nj, _ = a_ref.shape
    for slot in range(rows):
        r = slot % (rows // 2) * 2 + slot // (rows // 2)
        for i in range(ni):
            piece = jnp.concatenate([a_ref[i, k, :, r * sub : (r + 1) * sub] for k in range(nk)], axis=1)
            o_ref[slot, i * nj : (i + 1) * nj, :] = piece


def pack_b_kernel(p_ref, b_ref, keep_ref, send_ref):
    full = jnp.concatenate([b_ref[k] for k in range(b_ref.shape[0])], axis=1)
    half = full.shape[0] // 2
    pad = jnp.zeros((keep_ref.shape[0] - half, full.shape[1]), full.dtype)
    low = jnp.concatenate([full[:half], pad], axis=0)
    high = jnp.concatenate([full[half:], pad], axis=0)
    first = p_ref[0] == 0

    @pl.when(first)
    def _():
        keep_ref[...] = low
        send_ref[...] = high

    @pl.when(jnp.logical_not(first))
    def _():
        keep_ref[...] = high
        send_ref[...] = low


def join_kernel(x_ref, y_ref, o_ref):
    o_ref[0] = x_ref[...]
    o_ref[1] = y_ref[...]


def contract_kernel(half, count, core_ref, own0, own1, oth0, oth1, *refs):
    blocks, earlier, o_ref = refs[:count], refs[count:-1], refs[-1]
    core = core_ref[0]
    dims = (((1,), (1,)), ((), ()))
    rt, mi, kc = own0.shape
    for slot, pair in ((core, (own0, own1)), (1 - core, (oth0, oth1))):
        lhs = [ref[...].reshape(rt * mi, kc) for ref in pair]
        parts = [r[:, pl.ds(slot, 1)].reshape(rt * mi, r.shape[-1]) for r in earlier]
        for block in blocks:
            acc = lax.dot_general(lhs[0], block[0], dims, preferred_element_type=F32)
            acc += lax.dot_general(lhs[1], block[1], dims, preferred_element_type=F32)
            parts.append(acc[:, :half].astype(BF))
        full = parts[0] if len(parts) == 1 else jnp.concatenate(parts, axis=1)
        o_ref[:, pl.ds(slot, 1), :, :] = full.reshape(rt, 1, mi, full.shape[1])


def contract(core, amps, blocks, half, earlier=()):
    rt, mi, kc = amps[0].shape
    fresh = half * len(blocks)
    width = fresh + sum(e.shape[-1] for e in earlier)
    return pl.pallas_call(
        functools.partial(contract_kernel, half, len(blocks)),
        in_specs=[SM] + [VM] * (4 + len(blocks) + len(earlier)),
        out_specs=VM,
        out_shape=jax.ShapeDtypeStruct((rt, 2, mi, width), BF),
        cost_estimate=cost(2 * 2 * rt * mi * 2 * kc * fresh, 2 * (4 * rt * mi * kc + fresh * 2 * kc + 2 * rt * mi * width)),
        compiler_params=pltpu.CompilerParams(vmem_limit_bytes=24 << 20),
    )(core, *amps, *blocks, *earlier)


def total_kernel(half, x_ref, o_ref):
    sums = []
    for core in range(x_ref.shape[1]):
        acc = x_ref[0, core].astype(F32)
        for s in range(1, x_ref.shape[0]):
            acc += x_ref[s, core].astype(F32)
        sums.append(acc.astype(BF))
    for b in range(o_ref.shape[0]):
        o_ref[b] = jnp.concatenate([v[:, b * half : (b + 1) * half] for v in sums], axis=1)


def mask_kernel(y_ref, xh_ref, z_ref, core_ref, occ_ref, slab_ref, o_ref):
    target = slab_ref[0] ^ slab_ref[1]
    side = 4
    r = lax.broadcasted_iota(jnp.int32, o_ref.shape, 0)
    i_orb = (2 * y_ref[0] + xh_ref[0]) * side + r // side
    j_orb = (2 * z_ref[0] + core_ref[0]) * side + r % side
    i_lab = jnp.zeros(o_ref.shape, jnp.int32)
    j_lab = jnp.zeros(o_ref.shape, jnp.int32)
    for k in range(1, 8):
        i_lab += (i_orb >= occ_ref[k]).astype(jnp.int32)
        j_lab += (j_orb >= occ_ref[k]).astype(jnp.int32)
    o_ref[...] = ((i_lab ^ j_lab) == target).astype(jnp.int32)


def split_total_kernel(half, core_ref, x_ref, keep_ref, send_ref):
    for slot, o_ref in ((core_ref[0], keep_ref), (1 - core_ref[0], send_ref)):
        acc = x_ref[0, pl.ds(slot, 1)].astype(F32)
        for s in range(1, x_ref.shape[0]):
            acc += x_ref[s, pl.ds(slot, 1)].astype(F32)
        acc = acc[0].astype(BF)
        for b in range(o_ref.shape[0]):
            o_ref[b] = acc[:, b * half : (b + 1) * half]


def pair_kernel(core_ref, own_ref, oth_ref, o_ref):
    first = core_ref[0] == 0

    @pl.when(first)
    def _():
        o_ref[...] = jnp.concatenate([own_ref[...], oth_ref[...]], axis=2)

    @pl.when(jnp.logical_not(first))
    def _():
        o_ref[...] = jnp.concatenate([oth_ref[...], own_ref[...]], axis=2)


def antisym_kernel(layout, y_ref, z_ref, mask_ref, *refs):
    chunks = len(layout)
    s_refs, m_refs = refs[:chunks], refs[chunks : 2 * chunks]
    o_ref, s_all, m_all = refs[2 * chunks :]
    nz, n, _ = o_ref.shape
    for all_ref, parts, origin in ((s_all, s_refs, z_ref[0]), (m_all, m_refs, y_ref[0])):
        for offs, ref in zip(layout, parts):
            for b, off in enumerate(offs):
                all_ref[pl.ds(lax.rem(origin + off + nz, nz), 1)] = ref[b][None]
    side = 4
    ri = lax.broadcasted_iota(jnp.int32, (n, n), 0)
    ci = lax.broadcasted_iota(jnp.int32, (n, n), 1)
    swap = jnp.where((ri // side == ci % side) & (ri % side == ci // side), 1.0, 0.0).astype(BF)
    allowed = mask_ref[:, :1] > 0
    for z in range(nz):
        flipped = jnp.dot(swap, m_all[z], preferred_element_type=F32)
        mixed = s_all[z].astype(F32) - flipped
        o_ref[z] = jnp.where(allowed, mixed, 0.0).astype(BF)


def assemble_kernel(half, p_ref, own_ref, oth_ref, o_ref):
    first = p_ref[0] == 0
    nj = o_ref.shape[1]

    def write(low_ref, high_ref):
        for i in range(o_ref.shape[0]):
            rows = slice(i * nj, (i + 1) * nj)
            parts = [
                ref[z, rows, core * half : (core + 1) * half]
                for z in range(own_ref.shape[0])
                for core in range(2)
                for ref in (low_ref, high_ref)
            ]
            o_ref[i] = jnp.concatenate(parts, axis=1)

    @pl.when(first)
    def _():
        write(own_ref, oth_ref)

    @pl.when(jnp.logical_not(first))
    def _():
        write(oth_ref, own_ref)


def kernel_call(body, outs, in_specs, args, nbytes, scratch=()):
    many = isinstance(outs, (list, tuple))
    return pl.pallas_call(
        body,
        in_specs=in_specs,
        out_specs=[VM] * len(outs) if many else VM,
        out_shape=outs,
        scratch_shapes=scratch,
        cost_estimate=cost(nbytes, nbytes),
        compiler_params=pltpu.CompilerParams(vmem_limit_bytes=12 << 20),
    )(*args)


def residual_of(amplitudes, integrals, occ_offsets, slab):
    ni, nj, nk, nc = amplitudes.shape
    na, _, sub = integrals.shape
    rows = nc // sub
    half = na // 2
    kc = nk * sub

    def at(axis):
        return lax.axis_index(axis).astype(jnp.int32).reshape(1)

    def shift(x, axis, by):
        n = lax.axis_size(axis)
        return lax.ppermute(x, axis, [(d, (d + by) % n) for d in range(n)])

    padded = -(-half // 8) * 8
    keep, send = kernel_call(
        pack_b_kernel,
        [jax.ShapeDtypeStruct((padded, kc), BF)] * 2,
        [SM, VM],
        (at("xl"), jnp.transpose(integrals, (1, 0, 2))),
        4 * na * kc,
    )
    packed_a = kernel_call(
        functools.partial(pack_a_kernel, rows, sub),
        jax.ShapeDtypeStruct((rows, ni * nj, kc), BF),
        [VM],
        (jnp.transpose(amplitudes, (0, 2, 1, 3)),),
        4 * ni * nj * nk * nc,
    )
    recv = shift(send, "xl", 1)

    block = kernel_call(
        join_kernel,
        jax.ShapeDtypeStruct((2, padded, kc), BF),
        [VM, VM],
        (keep, recv),
        8 * padded * kc,
    )

    up, down = [block], [block]
    for t in range(1, 5):
        up.append(shift(up[-1], "z", 1))
        if t < 4:
            down.append(shift(down[-1], "z", -1))

    own0 = lax.all_to_all(packed_a, ROW, split_axis=0, concat_axis=0, tiled=True)
    own1 = shift(own0, "xl", 1)
    oth0 = shift(own0, "core", 1)
    oth1 = shift(own1, "core", 1)

    layout = ((0, -1, 1, -2, 2), (-3, 4, 3))
    where, amps = at("core"), (own0, own1, oth0, oth1)
    near = contract(where, amps, (block, up[1], down[1]), half)
    part_0 = contract(where, amps, (up[2], down[2]), half, (near,))
    early = contract(where, amps, (up[3], up[4]), half)
    part_1 = contract(where, amps, (down[3],), half, (early,))

    n = ni * nj
    shape = tuple(lax.axis_size(a) for a in AXES)
    pairs = []
    for at_y, at_xh, at_z, at_core, at_xl in np.ndindex(*shape):
        here, there = (at_y, at_xh, at_z, at_core, at_xl), (at_z, at_core, at_y, at_xh, at_xl)
        pairs.append((int(np.ravel_multi_index(here, shape)), int(np.ravel_multi_index(there, shape))))
    sums, mirrored = [], []
    blocks, width = len(layout[0]), part_0.shape[-1]
    part_0 = lax.all_to_all(part_0, ROW, split_axis=0, concat_axis=0, tiled=True)
    mine, theirs = kernel_call(
        functools.partial(split_total_kernel, half),
        [jax.ShapeDtypeStruct((blocks, n, half), BF)] * 2,
        [SM, VM],
        (where, part_0),
        4 * rows * n * width,
    )
    given = shift(theirs, "core", 1)
    sums.append(
        kernel_call(
            pair_kernel,
            jax.ShapeDtypeStruct((blocks, n, 2 * half), BF),
            [SM, VM, VM],
            (where, mine, given),
            8 * blocks * n * half,
        )
    )
    blocks, width = len(layout[1]), part_1.shape[-1]
    part_1 = part_1.reshape(rows * 2, n, width)
    part_1 = lax.all_to_all(part_1, TARGET, split_axis=0, concat_axis=0, tiled=True)
    part_1 = part_1.reshape(rows, 2, n, width)
    sums.append(
        kernel_call(
            functools.partial(total_kernel, half),
            jax.ShapeDtypeStruct((blocks, n, 2 * half), BF),
            [VM],
            (part_1,),
            4 * rows * n * width,
        )
    )
    for c in range(2):
        mirrored.append(lax.ppermute(sums[c], AXES, pairs))

    held = (lax.axis_size("z"), n, 2 * half)
    allowed = kernel_call(
        mask_kernel,
        jax.ShapeDtypeStruct((n, 128), jnp.int32),
        [SM] * 6,
        (at("y"), at("xh"), at("z"), at("core"), occ_offsets, slab),
        4 * n * 128,
    )
    mixed = kernel_call(
        functools.partial(antisym_kernel, layout),
        jax.ShapeDtypeStruct(held, BF),
        [SM] * 2 + [VM] * 5,
        (at("y"), at("z"), allowed, *sums, *mirrored),
        6 * int(np.prod(held)),
        [pltpu.VMEM(held, BF)] * 2,
    )
    other = shift(mixed, "xl", 1)
    return kernel_call(
        functools.partial(assemble_kernel, half),
        jax.ShapeDtypeStruct((ni, nj, held[0] * 4 * half), BF),
        [SM, VM, VM],
        (at("xl"), mixed, other),
        8 * int(np.prod(held)),
    )


def solution(mesh):
    fine = Mesh(mesh.devices.reshape(8, 2, 8, 2, 2), AXES)
    row, col = ("y", "xh"), ("z", "core")
    placed = (P(row, col, "xl", None), P(col, "xl", row), P(), P())
    return jax.shard_map(
        residual_of, mesh=fine, in_specs=placed, out_specs=P(row, col, None), check_vma=False
    )
```

time: 436 us -> 177 us (0.41)
  the two profiles are of different devices: /device:TPU:1 before, /device:TPU:44 now
where the time goes in v2:
time: 177 us; the launch traced here: 176 us
  waiting for transfers between devices  84 us (47%)
  starting transfers between devices  76.7 us (43%)
  Pallas kernels  13.5 us (8%)
    ppermute x13, waiting for transfers between devices, shift(): return lax.ppermute(x, axis, [(d, (d + by) % n) for d in range(n)])  61.9 us
    ppermute x13, starting transfers between devices, shift(): return lax.ppermute(x, axis, [(d, (d + by) % n) for d in range(n)])  43.9 us
    all_to_all x1, waiting for transfers between devices, residual_of(): lax.all_to_all(part_1, TARGET, split_axis=0, concat_axis=0, tiled=True)  11.5 us
    ppermute x2, waiting for transfers between devices, residual_of(): mirrored.append(lax.ppermute(sums[c], AXES, pairs))  10.7 us
    all_to_all x1, starting transfers between devices, residual_of(): lax.all_to_all(part_1, TARGET, split_axis=0, concat_axis=0, tiled=True)  9.83 us
    all_to_all x1, starting transfers between devices, residual_of(): lax.all_to_all(packed_a, ROW, split_axis=0, concat_axis=0, tiled=True)  9.65 us
    pallas_call x4, Pallas kernels, contract(): pl.pallas_call(functools.partial(contract_kernel, half, len(blocks)), in_...  9.49 us
    all_to_all x1, starting transfers between devices, residual_of(): lax.all_to_all(part_0, ROW, split_axis=0, concat_axis=0, tiled=True)  8.73 us
  transfers between devices with their start and end apart: 18, of which 12 were waited for; matrix products, arithmetic and copies ran while one was open for 0% of the time, Pallas kernels for 4%

profile of v2, /device:TPU:44, one launch (start us, length us, event | category | flops | bytes accessed | tf_op | source)
XLA Modules:
  0.0 176.1 jit_solution(17859816496878831923)
XLA Ops:
  0.0 0.0 copy-start.2
  0.0 1.0 copy-done.2
  1.0 1.5 shard_map.47
  2.6 0.0 copy-start
  2.6 9.6 %all-to-all-start = ((bf16[16,16,972]{2,1,0:T(8,128)(2,1)}), bf16[16,16,972]{2,1,0:T(8,128)(2,1)S(1)}, u32[]{:S(2)}, u32[]{:S(2)}) async-start(bf16[16,16,972]{2,1,0:T(8,128)(2,1)} %shard_map.47), calls=%async_computation | async-start | bytes 1048576 | tf_op jit(solution)/shard_map/all_to_all | solution.py:236
  12.2 0.0 copy-done
  12.2 0.2 shard_map.48
  12.5 3.1 %collective-permute-start.3 = (bf16[168,972]{1,0:T(8,128)(2,1)S(1)}, bf16[168,972]{1,0:T(8,128)(2,1)S(1)}, u32[]{:S(2)}, u32[]{:S(2)}) collective-permute-start(bf16[168,972]{1,0:T(8,128)(2,1)S(1)} %get-tuple-element.10), channel_id=1, source_target_pairs={{0,1},{1,0},{2,3},{3,2},{4,5},{5,4},{6,7},{7,6},{8,9},{9,8},{10,11... | collective-permute-start | bytes 979784 | tf_op jit(solution)/shard_map/ppermute | solution.py:203
  15.6 12.2 %collective-permute-done.3.y_ref = bf16[168,972]{1,0:T(8,128)(2,1)S(1)} collective-permute-done((bf16[168,972]{1,0:T(8,128)(2,1)S(1)}, bf16[168,972]{1,0:T(8,128)(2,1)S(1)}, u32[]{:S(2)}, u32[]{:S(2)}) %collective-permute-start.3) | collective-permute-done | bytes 326624 | tf_op jit(solution)/shard_map/ppermute | solution.py:203
  27.9 10.9 %collective-permute-start.6 = (bf16[2,168,972]{2,1,0:T(8,128)(2,1)S(1)}, bf16[2,168,972]{2,1,0:T(8,128)(2,1)}, u32[]{:S(2)}, u32[]{:S(2)}) collective-permute-start(bf16[2,168,972]{2,1,0:T(8,128)(2,1)S(1)} %shard_map.49.refs_0_), channel_id=1, source_target_pairs={{0,28},{4,0},{8,4},{12,8},{16,12},{20,16},{24,20},{28,24},{1,29},{... | collective-permute-start | bytes 1959560 | tf_op jit(solution)/shard_map/ppermute | solution.py:203
  38.8 1.9 %collective-permute-start.4 = (bf16[2,168,972]{2,1,0:T(8,128)(2,1)S(1)}, bf16[2,168,972]{2,1,0:T(8,128)(2,1)}, u32[]{:S(2)}, u32[]{:S(2)}) collective-permute-start(bf16[2,168,972]{2,1,0:T(8,128)(2,1)S(1)} %shard_map.49.refs_0_), channel_id=1, source_target_pairs={{0,4},{4,8},{8,12},{12,16},{16,20},{20,24},{24,28},{28,0},{1,5},{5... | collective-permute-start | bytes 1959560 | tf_op jit(solution)/shard_map/ppermute | solution.py:203
  40.8 0.0 all-to-all-done.own0
  40.8 2.9 %collective-permute-start = (bf16[16,16,972]{2,1,0:T(8,128)(2,1)S(1)}, bf16[16,16,972]{2,1,0:T(8,128)(2,1)S(1)}, u32[]{:S(2)}, u32[]{:S(2)}) collective-permute-start(bf16[16,16,972]{2,1,0:T(8,128)(2,1)S(1)} %all-to-all-done.own0), channel_id=1, source_target_pairs={{0,1},{1,0},{2,3},{3,2},{4,5},{5,4},{6,7},{7,6},{8,9},{9,8},{10,11... | collective-permute-start | bytes 1493000 | tf_op jit(solution)/shard_map/ppermute | solution.py:203
  43.7 9.4 %collective-permute-done.6.refs_2_ = bf16[2,168,972]{2,1,0:T(8,128)(2,1)} collective-permute-done((bf16[2,168,972]{2,1,0:T(8,128)(2,1)S(1)}, bf16[2,168,972]{2,1,0:T(8,128)(2,1)}, u32[]{:S(2)}, u32[]{:S(2)}) %collective-permute-start.6) | collective-permute-done | bytes 653216 | tf_op jit(solution)/shard_map/ppermute | solution.py:203
  53.1 5.7 %collective-permute-start.7 = (bf16[2,168,972]{2,1,0:T(8,128)(2,1)}, bf16[2,168,972]{2,1,0:T(8,128)(2,1)S(1)}, u32[]{:S(2)}, u32[]{:S(2)}) collective-permute-start(bf16[2,168,972]{2,1,0:T(8,128)(2,1)} %collective-permute-done.6.refs_2_), channel_id=1, source_target_pairs={{0,28},{4,0},{8,4},{12,8},{16,12},{20,16},{24,20},{28,24},{1,29},{... | collective-permute-start | bytes 1959560 | tf_op jit(solution)/shard_map/ppermute | solution.py:203
  58.8 0.0 collective-permute-done.4.refs_1_
  58.8 1.9 %collective-permute-start.5 = (bf16[2,168,972]{2,1,0:T(8,128)(2,1)}, bf16[2,168,972]{2,1,0:T(8,128)(2,1)}, u32[]{:S(2)}, u32[]{:S(2)}) collective-permute-start(bf16[2,168,972]{2,1,0:T(8,128)(2,1)} %collective-permute-done.4.refs_1_), channel_id=1, source_target_pairs={{0,4},{4,8},{8,12},{12,16},{16,20},{20,24},{24,28},{28,0},{1,5},{5... | collective-permute-start | bytes 1959560 | tf_op jit(solution)/shard_map/ppermute | solution.py:203
  60.8 1.9 %collective-permute-start.1 = (bf16[16,16,972]{2,1,0:T(8,128)(2,1)S(1)}, bf16[16,16,972]{2,1,0:T(8,128)(2,1)S(1)}, u32[]{:S(2)}, u32[]{:S(2)}) collective-permute-start(bf16[16,16,972]{2,1,0:T(8,128)(2,1)S(1)} %all-to-all-done.own0), channel_id=1, source_target_pairs={{0,2},{2,0},{1,3},{3,1},{4,6},{6,4},{5,7},{7,5},{8,10},{10,8},{9,1... | collective-permute-start | bytes 1493000 | tf_op jit(solution)/shard_map/ppermute | solution.py:203
  62.7 0.0 collective-permute-done.own1
  62.7 2.4 %collective-permute-start.2 = (bf16[16,16,972]{2,1,0:T(8,128)(2,1)S(1)}, bf16[16,16,972]{2,1,0:T(8,128)(2,1)S(1)}, u32[]{:S(2)}, u32[]{:S(2)}) collective-permute-start(bf16[16,16,972]{2,1,0:T(8,128)(2,1)S(1)} %collective-permute-done.own1), channel_id=1, source_target_pairs={{0,2},{2,0},{1,3},{3,1},{4,6},{6,4},{5,7},{7,5},{8,10},{10,8},{9,1... | collective-permute-start | bytes 1493000 | tf_op jit(solution)/shard_map/ppermute | solution.py:203
  65.1 0.0 collective-permute-done.1.oth0
  65.1 1.5 collective-permute-done.2.oth1
  66.6 3.2 %shard_map.50.refs_2_ = bf16[16,2,16,486]{3,2,1,0:T(8,128)(2,1)S(1)} custom-call(s32[1]{0:T(128)} %bitcast.4.core_ref, bf16[16,16,972]{2,1,0:T(8,128)(2,1)S(1)} %all-to-all-done.own0, bf16[16,16,972]{2,1,0:T(8,128)(2,1)S(1)} %collective-permute-done.own1, bf16[16,16,972]{2,1,0:T(8,128)(2,1)S(1)} %collective-permute-done.1.oth0, ...), custom_call_target="tpu_custom_call" | custom-call | flops 967458816 | bytes 4377888 | tf_op jit(solution)/shard_map/pallas_call | solution.py:77
  69.8 2.7 %collective-permute-done.7.refs_1_ = bf16[2,168,972]{2,1,0:T(8,128)(2,1)S(1)} collective-permute-done((bf16[2,168,972]{2,1,0:T(8,128)(2,1)}, bf16[2,168,972]{2,1,0:T(8,128)(2,1)S(1)}, u32[]{:S(2)}, u32[]{:S(2)}) %collective-permute-start.7) | collective-permute-done | bytes 653216 | tf_op jit(solution)/shard_map/ppermute | solution.py:203
  72.5 0.0 copy-start.1
  72.5 5.3 %collective-permute-done.5.refs_0_ = bf16[2,168,972]{2,1,0:T(8,128)(2,1)} collective-permute-done((bf16[2,168,972]{2,1,0:T(8,128)(2,1)}, bf16[2,168,972]{2,1,0:T(8,128)(2,1)}, u32[]{:S(2)}, u32[]{:S(2)}) %collective-permute-start.5) | collective-permute-done | bytes 653216 | tf_op jit(solution)/shard_map/ppermute | solution.py:203
  77.9 3.4 %shard_map.51 = bf16[16,2,16,810]{3,2,1,0:T(8,128)(2,1)} custom-call(s32[1]{0:T(128)} %bitcast.4.core_ref, bf16[16,16,972]{2,1,0:T(8,128)(2,1)S(1)} %all-to-all-done.own0, bf16[16,16,972]{2,1,0:T(8,128)(2,1)S(1)} %collective-permute-done.own1, bf16[16,16,972]{2,1,0:T(8,128)(2,1)S(1)} %collective-permute-done.1.oth0, ...), custom_call_target="tpu_custom_call" | custom-call | flops 644972544 | bytes 4079808 | tf_op jit(solution)/shard_map/pallas_call | solution.py:77
  81.2 0.0 copy-done.1
  81.2 8.7 %all-to-all-start.1 = ((bf16[16,2,16,810]{3,2,1,0:T(8,128)(2,1)}), bf16[16,2,16,810]{3,2,1,0:T(8,128)(2,1)S(1)}, u32[]{:S(2)}, u32[]{:S(2)}) async-start(bf16[16,2,16,810]{3,2,1,0:T(8,128)(2,1)} %shard_map.51), calls=%async_computation.1 | async-start | bytes 1835008 | tf_op jit(solution)/shard_map/all_to_all | solution.py:256
  90.0 1.9 %collective-permute-start.10 = (bf16[2,168,972]{2,1,0:T(8,128)(2,1)}, bf16[2,168,972]{2,1,0:T(8,128)(2,1)S(1)}, u32[]{:S(2)}, u32[]{:S(2)}) collective-permute-start(bf16[2,168,972]{2,1,0:T(8,128)(2,1)} %collective-permute-done.5.refs_0_), channel_id=1, source_target_pairs={{0,4},{4,8},{8,12},{12,16},{16,20},{20,24},{24,28},{28,0},{1,5},{5... | collective-permute-start | bytes 1959560 | tf_op jit(solution)/shard_map/ppermute | solution.py:203
  91.9 15.6 %collective-permute-done.10.refs_0_ = bf16[2,168,972]{2,1,0:T(8,128)(2,1)S(1)} collective-permute-done((bf16[2,168,972]{2,1,0:T(8,128)(2,1)}, bf16[2,168,972]{2,1,0:T(8,128)(2,1)S(1)}, u32[]{:S(2)}, u32[]{:S(2)}) %collective-permute-start.10) | collective-permute-done | bytes 653216 | tf_op jit(solution)/shard_map/ppermute | solution.py:203
  107.5 1.9 %collective-permute-start.11 = (bf16[2,168,972]{2,1,0:T(8,128)(2,1)S(1)}, bf16[2,168,972]{2,1,0:T(8,128)(2,1)S(1)}, u32[]{:S(2)}, u32[]{:S(2)}) collective-permute-start(bf16[2,168,972]{2,1,0:T(8,128)(2,1)S(1)} %collective-permute-done.10.refs_0_), channel_id=1, source_target_pairs={{0,4},{4,8},{8,12},{12,16},{16,20},{20,24},{24,28},{28,0},{1,5},{5... | collective-permute-start | bytes 1959560 | tf_op jit(solution)/shard_map/ppermute | solution.py:203
  109.4 5.1 %collective-permute-start.9 = (bf16[2,168,972]{2,1,0:T(8,128)(2,1)}, bf16[2,168,972]{2,1,0:T(8,128)(2,1)S(1)}, u32[]{:S(2)}, u32[]{:S(2)}) collective-permute-start(bf16[2,168,972]{2,1,0:T(8,128)(2,1)} %copy-done.1), channel_id=1, source_target_pairs={{0,28},{4,0},{8,4},{12,8},{16,12},{20,16},{24,20},{28,24},{1,29},{... | collective-permute-start | bytes 1959560 | tf_op jit(solution)/shard_map/ppermute | solution.py:203
  114.6 9.4 %collective-permute-done.11.refs_1_ = bf16[2,168,972]{2,1,0:T(8,128)(2,1)S(1)} collective-permute-done((bf16[2,168,972]{2,1,0:T(8,128)(2,1)S(1)}, bf16[2,168,972]{2,1,0:T(8,128)(2,1)S(1)}, u32[]{:S(2)}, u32[]{:S(2)}) %collective-permute-start.11) | collective-permute-done | bytes 653216 | tf_op jit(solution)/shard_map/ppermute | solution.py:203
  123.9 1.3 shard_map.54.refs_1_
  125.3 0.2 collective-permute-done.9.refs_0_
  125.4 1.6 shard_map.55
  127.1 0.0 all-to-all-done.1.x_ref
  127.1 9.8 %all-to-all-start.2 = ((bf16[32,16,486]{2,1,0:T(8,128)(2,1)}), bf16[32,16,486]{2,1,0:T(8,128)(2,1)S(1)}, u32[]{:S(2)}, u32[]{:S(2)}) async-start(bf16[32,16,486]{2,1,0:T(8,128)(2,1)} %bitcast.7), calls=%async_computation.2 | async-start | bytes 1048576 | tf_op jit(solution)/shard_map/all_to_all | solution.py:276
  136.9 0.2 shard_map.52
  137.1 2.0 %collective-permute-start.8 = (bf16[5,16,162]{2,1,0:T(8,128)(2,1)S(1)}, bf16[5,16,162]{2,1,0:T(8,128)(2,1)S(1)}, u32[]{:S(2)}, u32[]{:S(2)}) collective-permute-start(bf16[5,16,162]{2,1,0:T(8,128)(2,1)S(1)} %get-tuple-element.12), channel_id=1, source_target_pairs={{0,2},{2,0},{1,3},{3,1},{4,6},{6,4},{5,7},{7,5},{8,10},{10,8},{9,1... | collective-permute-start | bytes 77768 | tf_op jit(solution)/shard_map/ppermute | solution.py:203
  139.1 1.1 collective-permute-done.8.oth_ref
  140.2 0.1 shard_map.53.refs_0_
  140.3 1.9 %collective-permute-start.12 = (bf16[5,16,324]{2,1,0:T(8,128)(2,1)S(1)}, bf16[5,16,324]{2,1,0:T(8,128)(2,1)S(1)}, u32[]{:S(2)}, u32[]{:S(2)}) collective-permute-start(bf16[5,16,324]{2,1,0:T(8,128)(2,1)S(1)} %shard_map.53.refs_0_), channel_id=1, source_target_pairs={{0,0},{1,1},{2,32},{3,33},{4,64},{5,65},{6,96},{7,97},{8,128},{9,1... | collective-permute-start | bytes 155528 | tf_op jit(solution)/shard_map/ppermute | solution.py:288
  142.2 11.5 %all-to-all-done.2 = bf16[32,16,486]{2,1,0:T(8,128)(2,1)S(1)} async-done(((bf16[32,16,486]{2,1,0:T(8,128)(2,1)}), bf16[32,16,486]{2,1,0:T(8,128)(2,1)S(1)}, u32[]{:S(2)}, u32[]{:S(2)}) %all-to-all-start.2) | async-done | bytes 497696 | tf_op jit(solution)/shard_map/all_to_all | solution.py:276
  153.7 0.1 shard_map.56.refs_1_
  153.8 2.7 %collective-permute-start.13 = (bf16[3,16,324]{2,1,0:T(8,128)(2,1)S(1)}, bf16[3,16,324]{2,1,0:T(8,128)(2,1)S(1)}, u32[]{:S(2)}, u32[]{:S(2)}) collective-permute-start(bf16[3,16,324]{2,1,0:T(8,128)(2,1)S(1)} %shard_map.56.refs_1_), channel_id=1, source_target_pairs={{0,0},{1,1},{2,32},{3,33},{4,64},{5,65},{6,96},{7,97},{8,128},{9,1... | collective-permute-start | bytes 93320 | tf_op jit(solution)/shard_map/ppermute | solution.py:288
  156.5 0.0 copy-start.3
  156.5 0.0 copy-start.4
  156.5 0.6 copy-done.3
  157.2 0.0 copy-done.4
  157.2 0.6 shard_map.46.mask_ref
  157.8 0.0 collective-permute-done.12.refs_2_
  157.8 10.7 %collective-permute-done.13.refs_3_ = bf16[3,16,324]{2,1,0:T(8,128)(2,1)S(1)} collective-permute-done((bf16[3,16,324]{2,1,0:T(8,128)(2,1)S(1)}, bf16[3,16,324]{2,1,0:T(8,128)(2,1)S(1)}, u32[]{:S(2)}, u32[]{:S(2)}) %collective-permute-start.13) | collective-permute-done | bytes 31136 | tf_op jit(solution)/shard_map/ppermute | solution.py:288
  168.4 0.2 shard_map.57.own_ref
  168.6 2.1 %collective-permute-start.14 = (bf16[8,16,324]{2,1,0:T(8,128)(2,1)S(1)}, bf16[8,16,324]{2,1,0:T(8,128)(2,1)S(1)}, u32[]{:S(2)}, u32[]{:S(2)}) collective-permute-start(bf16[8,16,324]{2,1,0:T(8,128)(2,1)S(1)} %shard_map.57.own_ref), channel_id=1, source_target_pairs={{0,1},{1,0},{2,3},{3,2},{4,5},{5,4},{6,7},{7,6},{8,9},{9,8},{10,11... | collective-permute-start | bytes 248840 | tf_op jit(solution)/shard_map/ppermute | solution.py:203
  170.7 4.4 %collective-permute-done.14.oth_ref = bf16[8,16,324]{2,1,0:T(8,128)(2,1)S(1)} collective-permute-done((bf16[8,16,324]{2,1,0:T(8,128)(2,1)S(1)}, bf16[8,16,324]{2,1,0:T(8,128)(2,1)S(1)}, u32[]{:S(2)}, u32[]{:S(2)}) %collective-permute-start.14) | collective-permute-done | bytes 82976 | tf_op jit(solution)/shard_map/ppermute | solution.py:203
  175.1 1.0 shard_map.58
  (1 shorter events, 0.0 us)
Async XLA Ops:
  0.0 1.0 copy-start.2
  2.6 9.7 %copy-start = (bf16[324,3,324]{2,0,1:T(8,128)(2,1)S(1)}, bf16[324,3,324]{2,0,1:T(8,128)(2,1)}, u32[]{:S(2)}) copy-start(bf16[324,3,324]{2,0,1:T(8,128)(2,1)} %param.5) | copy-start | bytes 1889572
  2.6 38.2 %all-to-all-start = ((bf16[16,16,972]{2,1,0:T(8,128)(2,1)}), bf16[16,16,972]{2,1,0:T(8,128)(2,1)S(1)}, u32[]{:S(2)}, u32[]{:S(2)}) async-start(bf16[16,16,972]{2,1,0:T(8,128)(2,1)} %shard_map.47), calls=%async_computation | async-start | bytes 1048576 | tf_op jit(solution)/shard_map/all_to_all | solution.py:236
  12.5 15.4 %collective-permute-start.3 = (bf16[168,972]{1,0:T(8,128)(2,1)S(1)}, bf16[168,972]{1,0:T(8,128)(2,1)S(1)}, u32[]{:S(2)}, u32[]{:S(2)}) collective-permute-start(bf16[168,972]{1,0:T(8,128)(2,1)S(1)} %get-tuple-element.10), channel_id=1, source_target_pairs={{0,1},{1,0},{2,3},{3,2},{4,5},{5,4},{6,7},{7,6},{8,9},{9,8},{10,11... | collective-permute-start | bytes 979784 | tf_op jit(solution)/shard_map/ppermute | solution.py:203
  27.9 25.2 %collective-permute-start.6 = (bf16[2,168,972]{2,1,0:T(8,128)(2,1)S(1)}, bf16[2,168,972]{2,1,0:T(8,128)(2,1)}, u32[]{:S(2)}, u32[]{:S(2)}) collective-permute-start(bf16[2,168,972]{2,1,0:T(8,128)(2,1)S(1)} %shard_map.49.refs_0_), channel_id=1, source_target_pairs={{0,28},{4,0},{8,4},{12,8},{16,12},{20,16},{24,20},{28,24},{1,29},{... | collective-permute-start | bytes 1959560 | tf_op jit(solution)/shard_map/ppermute | solution.py:203
  38.8 20.0 %collective-permute-start.4 = (bf16[2,168,972]{2,1,0:T(8,128)(2,1)S(1)}, bf16[2,168,972]{2,1,0:T(8,128)(2,1)}, u32[]{:S(2)}, u32[]{:S(2)}) collective-permute-start(bf16[2,168,972]{2,1,0:T(8,128)(2,1)S(1)} %shard_map.49.refs_0_), channel_id=1, source_target_pairs={{0,4},{4,8},{8,12},{12,16},{16,20},{20,24},{24,28},{28,0},{1,5},{5... | collective-permute-start | bytes 1959560 | tf_op jit(solution)/shard_map/ppermute | solution.py:203
  40.8 21.9 %collective-permute-start = (bf16[16,16,972]{2,1,0:T(8,128)(2,1)S(1)}, bf16[16,16,972]{2,1,0:T(8,128)(2,1)S(1)}, u32[]{:S(2)}, u32[]{:S(2)}) collective-permute-start(bf16[16,16,972]{2,1,0:T(8,128)(2,1)S(1)} %all-to-all-done.own0), channel_id=1, source_target_pairs={{0,1},{1,0},{2,3},{3,2},{4,5},{5,4},{6,7},{7,6},{8,9},{9,8},{10,11... | collective-permute-start | bytes 1493000 | tf_op jit(solution)/shard_map/ppermute | solution.py:203
  53.1 19.4 %collective-permute-start.7 = (bf16[2,168,972]{2,1,0:T(8,128)(2,1)}, bf16[2,168,972]{2,1,0:T(8,128)(2,1)S(1)}, u32[]{:S(2)}, u32[]{:S(2)}) collective-permute-start(bf16[2,168,972]{2,1,0:T(8,128)(2,1)} %collective-permute-done.6.refs_2_), channel_id=1, source_target_pairs={{0,28},{4,0},{8,4},{12,8},{16,12},{20,16},{24,20},{28,24},{1,29},{... | collective-permute-start | bytes 1959560 | tf_op jit(solution)/shard_map/ppermute | solution.py:203
  58.8 19.1 %collective-permute-start.5 = (bf16[2,168,972]{2,1,0:T(8,128)(2,1)}, bf16[2,168,972]{2,1,0:T(8,128)(2,1)}, u32[]{:S(2)}, u32[]{:S(2)}) collective-permute-start(bf16[2,168,972]{2,1,0:T(8,128)(2,1)} %collective-permute-done.4.refs_1_), channel_id=1, source_target_pairs={{0,4},{4,8},{8,12},{12,16},{16,20},{20,24},{24,28},{28,0},{1,5},{5... | collective-permute-start | bytes 1959560 | tf_op jit(solution)/shard_map/ppermute | solution.py:203
  60.8 4.4 %collective-permute-start.1 = (bf16[16,16,972]{2,1,0:T(8,128)(2,1)S(1)}, bf16[16,16,972]{2,1,0:T(8,128)(2,1)S(1)}, u32[]{:S(2)}, u32[]{:S(2)}) collective-permute-start(bf16[16,16,972]{2,1,0:T(8,128)(2,1)S(1)} %all-to-all-done.own0), channel_id=1, source_target_pairs={{0,2},{2,0},{1,3},{3,1},{4,6},{6,4},{5,7},{7,5},{8,10},{10,8},{9,1... | collective-permute-start | bytes 1493000 | tf_op jit(solution)/shard_map/ppermute | solution.py:203
  62.7 3.9 %collective-permute-start.2 = (bf16[16,16,972]{2,1,0:T(8,128)(2,1)S(1)}, bf16[16,16,972]{2,1,0:T(8,128)(2,1)S(1)}, u32[]{:S(2)}, u32[]{:S(2)}) collective-permute-start(bf16[16,16,972]{2,1,0:T(8,128)(2,1)S(1)} %collective-permute-done.own1), channel_id=1, source_target_pairs={{0,2},{2,0},{1,3},{3,1},{4,6},{6,4},{5,7},{7,5},{8,10},{10,8},{9,1... | collective-permute-start | bytes 1493000 | tf_op jit(solution)/shard_map/ppermute | solution.py:203
  72.5 8.7 %copy-start.1 = (bf16[2,168,972]{2,1,0:T(8,128)(2,1)}, bf16[2,168,972]{2,1,0:T(8,128)(2,1)S(1)}, u32[]{:S(2)}) copy-start(bf16[2,168,972]{2,1,0:T(8,128)(2,1)S(1)} %collective-permute-done.7.refs_1_) | copy-start | bytes 1959556
  81.2 45.8 %all-to-all-start.1 = ((bf16[16,2,16,810]{3,2,1,0:T(8,128)(2,1)}), bf16[16,2,16,810]{3,2,1,0:T(8,128)(2,1)S(1)}, u32[]{:S(2)}, u32[]{:S(2)}) async-start(bf16[16,2,16,810]{3,2,1,0:T(8,128)(2,1)} %shard_map.51), calls=%async_computation.1 | async-start | bytes 1835008 | tf_op jit(solution)/shard_map/all_to_all | solution.py:256
  90.0 17.5 %collective-permute-start.10 = (bf16[2,168,972]{2,1,0:T(8,128)(2,1)}, bf16[2,168,972]{2,1,0:T(8,128)(2,1)S(1)}, u32[]{:S(2)}, u32[]{:S(2)}) collective-permute-start(bf16[2,168,972]{2,1,0:T(8,128)(2,1)} %collective-permute-done.5.refs_0_), channel_id=1, source_target_pairs={{0,4},{4,8},{8,12},{12,16},{16,20},{20,24},{24,28},{28,0},{1,5},{5... | collective-permute-start | bytes 1959560 | tf_op jit(solution)/shard_map/ppermute | solution.py:203
  107.5 16.4 %collective-permute-start.11 = (bf16[2,168,972]{2,1,0:T(8,128)(2,1)S(1)}, bf16[2,168,972]{2,1,0:T(8,128)(2,1)S(1)}, u32[]{:S(2)}, u32[]{:S(2)}) collective-permute-start(bf16[2,168,972]{2,1,0:T(8,128)(2,1)S(1)} %collective-permute-done.10.refs_0_), channel_id=1, source_target_pairs={{0,4},{4,8},{8,12},{12,16},{16,20},{20,24},{24,28},{28,0},{1,5},{5... | collective-permute-start | bytes 1959560 | tf_op jit(solution)/shard_map/ppermute | solution.py:203
  109.4 16.0 %collective-permute-start.9 = (bf16[2,168,972]{2,1,0:T(8,128)(2,1)}, bf16[2,168,972]{2,1,0:T(8,128)(2,1)S(1)}, u32[]{:S(2)}, u32[]{:S(2)}) collective-permute-start(bf16[2,168,972]{2,1,0:T(8,128)(2,1)} %copy-done.1), channel_id=1, source_target_pairs={{0,28},{4,0},{8,4},{12,8},{16,12},{20,16},{24,20},{28,24},{1,29},{... | collective-permute-start | bytes 1959560 | tf_op jit(solution)/shard_map/ppermute | solution.py:203
  127.1 26.6 %all-to-all-start.2 = ((bf16[32,16,486]{2,1,0:T(8,128)(2,1)}), bf16[32,16,486]{2,1,0:T(8,128)(2,1)S(1)}, u32[]{:S(2)}, u32[]{:S(2)}) async-start(bf16[32,16,486]{2,1,0:T(8,128)(2,1)} %bitcast.7), calls=%async_computation.2 | async-start | bytes 1048576 | tf_op jit(solution)/shard_map/all_to_all | solution.py:276
  137.1 3.1 %collective-permute-start.8 = (bf16[5,16,162]{2,1,0:T(8,128)(2,1)S(1)}, bf16[5,16,162]{2,1,0:T(8,128)(2,1)S(1)}, u32[]{:S(2)}, u32[]{:S(2)}) collective-permute-start(bf16[5,16,162]{2,1,0:T(8,128)(2,1)S(1)} %get-tuple-element.12), channel_id=1, source_target_pairs={{0,2},{2,0},{1,3},{3,1},{4,6},{6,4},{5,7},{7,5},{8,10},{10,8},{9,1... | collective-permute-start | bytes 77768 | tf_op jit(solution)/shard_map/ppermute | solution.py:203
  140.3 17.5 %collective-permute-start.12 = (bf16[5,16,324]{2,1,0:T(8,128)(2,1)S(1)}, bf16[5,16,324]{2,1,0:T(8,128)(2,1)S(1)}, u32[]{:S(2)}, u32[]{:S(2)}) collective-permute-start(bf16[5,16,324]{2,1,0:T(8,128)(2,1)S(1)} %shard_map.53.refs_0_), channel_id=1, source_target_pairs={{0,0},{1,1},{2,32},{3,33},{4,64},{5,65},{6,96},{7,97},{8,128},{9,1... | collective-permute-start | bytes 155528 | tf_op jit(solution)/shard_map/ppermute | solution.py:288
  153.8 14.6 %collective-permute-start.13 = (bf16[3,16,324]{2,1,0:T(8,128)(2,1)S(1)}, bf16[3,16,324]{2,1,0:T(8,128)(2,1)S(1)}, u32[]{:S(2)}, u32[]{:S(2)}) collective-permute-start(bf16[3,16,324]{2,1,0:T(8,128)(2,1)S(1)} %shard_map.56.refs_1_), channel_id=1, source_target_pairs={{0,0},{1,1},{2,32},{3,33},{4,64},{5,65},{6,96},{7,97},{8,128},{9,1... | collective-permute-start | bytes 93320 | tf_op jit(solution)/shard_map/ppermute | solution.py:288
  156.5 0.7 copy-start.3
  156.5 0.7 copy-start.4
  168.6 6.5 %collective-permute-start.14 = (bf16[8,16,324]{2,1,0:T(8,128)(2,1)S(1)}, bf16[8,16,324]{2,1,0:T(8,128)(2,1)S(1)}, u32[]{:S(2)}, u32[]{:S(2)}) collective-permute-start(bf16[8,16,324]{2,1,0:T(8,128)(2,1)S(1)} %shard_map.57.own_ref), channel_id=1, source_target_pairs={{0,1},{1,0},{2,3},{3,2},{4,5},{5,4},{6,7},{7,6},{8,9},{9,8},{10,11... | collective-permute-start | bytes 248840 | tf_op jit(solution)/shard_map/ppermute | solution.py:203

commit v3 on v2

--- a/solution.py
+++ b/solution.py
@@ -49,9 +49,41 @@
         send_ref[...] = low
 
 
-def join_kernel(x_ref, y_ref, o_ref):
-    o_ref[0] = x_ref[...]
-    o_ref[1] = y_ref[...]
+def block_plan(half, kc):
+    whole = kc // 128 * 128
+    second = 128 - kc % 128
+    left = kc - whole - second
+    top = half // 8 * 8
+    spare = top + 8 - half
+    return whole, second, left, top, spare
+
+
+def spread(half, kc, first_axis):
+    _, _, left, _, spare = block_plan(half, kc)
+    slots = -(-left // spare) * 8
+    shape = (left, slots) if first_axis else (slots, left)
+    source = lax.broadcasted_iota(jnp.int32, shape, 0 if first_axis else 1)
+    slot = lax.broadcasted_iota(jnp.int32, shape, 1 if first_axis else 0)
+    hit = slot == source // spare * 8 + (8 - spare) + source % spare
+    return jnp.where(hit, 1.0, 0.0).astype(BF)
+
+
+def join_kernel(half, x_ref, y_ref, o_ref):
+    rows, kc = x_ref.shape
+    whole, second, _, top, _ = block_plan(half, kc)
+    wide = whole + second
+    x, y = x_ref[...], y_ref[...]
+    main = jnp.concatenate([x, y[:, whole:wide], y[:, :whole]], axis=1)
+    o_ref[:top] = main[:top]
+    dims = (((1,), (1,)), ((), ()))
+    turned = lax.dot_general(spread(half, kc, False), y[:, wide:], dims, preferred_element_type=F32)
+    bottom = main[top:].astype(F32)
+    gap = jnp.zeros((8, -rows % 128), F32)
+    parts = []
+    for g in range(turned.shape[0] // 8):
+        parts += [turned[g * 8 : (g + 1) * 8], gap]
+    parts.append(jnp.zeros((8, main.shape[1] - sum(v.shape[1] for v in parts)), F32))
+    o_ref[top:] = (bottom + jnp.concatenate(parts, axis=1)).astype(BF)
 
 
 def contract_kernel(half, count, core_ref, own0, own1, oth0, oth1, *refs):
@@ -59,12 +91,23 @@
     core = core_ref[0]
     dims = (((1,), (1,)), ((), ()))
     rt, mi, kc = own0.shape
+    whole, second, left, top, spare = block_plan(half, kc)
+    wide = whole + second
+    rows = top + 8
+    step = rows + -rows % 128
+    groups = -(-left // spare)
     for slot, pair in ((core, (own0, own1)), (1 - core, (oth0, oth1))):
-        lhs = [ref[...].reshape(rt * mi, kc) for ref in pair]
+        lhs0, lhs1 = [ref[...].reshape(rt * mi, kc) for ref in pair]
+        front = jnp.concatenate([lhs0, lhs1[:, whole:wide]], axis=1)
+        back = lhs1[:, :whole]
+        last = jnp.dot(lhs1[:, wide:], spread(half, kc, True), preferred_element_type=F32).astype(BF)
         parts = [r[:, pl.ds(slot, 1)].reshape(rt * mi, r.shape[-1]) for r in earlier]
         for block in blocks:
-            acc = lax.dot_general(lhs[0], block[0], dims, preferred_element_type=F32)
-            acc += lax.dot_general(lhs[1], block[1], dims, preferred_element_type=F32)
+            turned = [block[top:, g * step : g * step + rows].astype(F32) for g in range(groups)]
+            turned = jnp.concatenate(turned, axis=0).astype(BF)
+            acc = lax.dot_general(front, block[:, : whole + 128], dims, preferred_element_type=F32)
+            acc += lax.dot_general(back, block[:, whole + 128 :], dims, preferred_element_type=F32)
+            acc += jnp.dot(last, turned, preferred_element_type=F32)
             parts.append(acc[:, :half].astype(BF))
         full = parts[0] if len(parts) == 1 else jnp.concatenate(parts, axis=1)
         o_ref[:, pl.ds(slot, 1), :, :] = full.reshape(rt, 1, mi, full.shape[1])
@@ -220,8 +263,8 @@
     recv = shift(send, "xl", 1)
 
     block = kernel_call(
-        join_kernel,
-        jax.ShapeDtypeStruct((2, padded, kc), BF),
+        functools.partial(join_kernel, half),
+        jax.ShapeDtypeStruct((padded, 2 * (kc // 128 * 128) + 128), BF),
         [VM, VM],
         (keep, recv),
         8 * padded * kc,
@@ -238,12 +281,12 @@
     oth0 = shift(own0, "core", 1)
     oth1 = shift(own1, "core", 1)
 
-    layout = ((0, -1, 1, -2, 2), (-3, 4, 3))
+    layout = ((0, -1, 1, -2, 2), (-3, 3, 4))
     where, amps = at("core"), (own0, own1, oth0, oth1)
     near = contract(where, amps, (block, up[1], down[1]), half)
     part_0 = contract(where, amps, (up[2], down[2]), half, (near,))
-    early = contract(where, amps, (up[3], up[4]), half)
-    part_1 = contract(where, amps, (down[3],), half, (early,))
+    early = contract(where, amps, (up[3], down[3]), half)
+    part_1 = contract(where, amps, (up[4],), half, (early,))
 
     n = ni * nj
     shape = tuple(lax.axis_size(a) for a in AXES)

time: 177 us -> 172 us (0.972)
  waiting for transfers between devices: 84 us -> 79.1 us
    ppermute x13, waiting for transfers between devices: 61.9 us -> 56.2 us  [shift(): return lax.ppermute(x, axis, [(d, (d + by) % n) for d in range(n)])]
  transfers between devices with their start and end apart: 18 -> 18, of which waited for: 12 -> 11; matrix products, arithmetic and copies ran while one was open for 0% -> 0% of each run, Pallas kernels for 4% -> 5%
where the time goes in v3:
time: 172 us
  waiting for transfers between devices  79.1 us (46%)
  starting transfers between devices  75.9 us (44%)
  Pallas kernels  13.6 us (8%)
  local copies, waits for them, and re-layouts  2.65 us (2%)
    ppermute x13, waiting for transfers between devices, shift(): return lax.ppermute(x, axis, [(d, (d + by) % n) for d in range(n)])  56.2 us
    ppermute x13, starting transfers between devices, shift(): return lax.ppermute(x, axis, [(d, (d + by) % n) for d in range(n)])  43.9 us
    all_to_all x1, waiting for transfers between devices, residual_of(): lax.all_to_all(part_1, TARGET, split_axis=0, concat_axis=0, tiled=True)  11.5 us
    ppermute x2, waiting for transfers between devices, residual_of(): mirrored.append(lax.ppermute(sums[c], AXES, pairs))  11.4 us
    all_to_all x1, starting transfers between devices, residual_of(): lax.all_to_all(part_1, TARGET, split_axis=0, concat_axis=0, tiled=True)  9.82 us
    all_to_all x1, starting transfers between devices, residual_of(): lax.all_to_all(packed_a, ROW, split_axis=0, concat_axis=0, tiled=True)  9.65 us
    pallas_call x4, Pallas kernels, contract(): pl.pallas_call(functools.partial(contract_kernel, half, len(blocks)), in_...  9.42 us
    all_to_all x1, starting transfers between devices, residual_of(): lax.all_to_all(part_0, ROW, split_axis=0, concat_axis=0, tiled=True)  8.73 us
  transfers between devices with their start and end apart: 18, of which 11 were waited for; matrix products, arithmetic and copies ran while one was open for 0% of the time, Pallas kernels for 5%

profile of v3, /device:TPU:44, one launch (start us, length us, event | category | flops | bytes accessed | tf_op | source)
XLA Modules:
  0.0 171.6 jit_solution(13727946112830708050)
XLA Ops:
  0.0 0.0 copy-start.3
  0.0 1.0 copy-done.3
  1.0 1.5 shard_map.47
  2.6 0.0 copy-start.1
  2.6 9.6 %all-to-all-start = ((bf16[16,16,972]{2,1,0:T(8,128)(2,1)}), bf16[16,16,972]{2,1,0:T(8,128)(2,1)S(1)}, u32[]{:S(2)}, u32[]{:S(2)}) async-start(bf16[16,16,972]{2,1,0:T(8,128)(2,1)} %shard_map.47), calls=%async_computation | async-start | bytes 1048576 | tf_op jit(solution)/shard_map/all_to_all | solution.py:279
  12.2 0.0 copy-done.1
  12.2 0.2 shard_map.48
  12.5 3.1 %collective-permute-start.3 = (bf16[168,972]{1,0:T(8,128)(2,1)S(1)}, bf16[168,972]{1,0:T(8,128)(2,1)S(1)}, u32[]{:S(2)}, u32[]{:S(2)}) collective-permute-start(bf16[168,972]{1,0:T(8,128)(2,1)S(1)} %get-tuple-element.10), channel_id=1, source_target_pairs={{0,1},{1,0},{2,3},{3,2},{4,5},{5,4},{6,7},{7,6},{8,9},{9,8},{10,11... | collective-permute-start | bytes 979784 | tf_op jit(solution)/shard_map/ppermute | solution.py:246
  15.6 12.2 %collective-permute-done.3.y_ref = bf16[168,972]{1,0:T(8,128)(2,1)S(1)} collective-permute-done((bf16[168,972]{1,0:T(8,128)(2,1)S(1)}, bf16[168,972]{1,0:T(8,128)(2,1)S(1)}, u32[]{:S(2)}, u32[]{:S(2)}) %collective-permute-start.3) | collective-permute-done | bytes 326624 | tf_op jit(solution)/shard_map/ppermute | solution.py:246
  27.8 0.2 shard_map.49.refs_0_
  28.1 11.0 %collective-permute-start.6 = (bf16[168,1920]{1,0:T(8,128)(2,1)S(1)}, bf16[168,1920]{1,0:T(8,128)(2,1)}, u32[]{:S(2)}, u32[]{:S(2)}) collective-permute-start(bf16[168,1920]{1,0:T(8,128)(2,1)S(1)} %shard_map.49.refs_0_), channel_id=1, source_target_pairs={{0,28},{4,0},{8,4},{12,8},{16,12},{20,16},{24,20},{28,24},{1,29},{... | collective-permute-start | bytes 1935368 | tf_op jit(solution)/shard_map/ppermute | solution.py:246
  39.0 1.9 %collective-permute-start.4 = (bf16[168,1920]{1,0:T(8,128)(2,1)S(1)}, bf16[168,1920]{1,0:T(8,128)(2,1)}, u32[]{:S(2)}, u32[]{:S(2)}) collective-permute-start(bf16[168,1920]{1,0:T(8,128)(2,1)S(1)} %shard_map.49.refs_0_), channel_id=1, source_target_pairs={{0,4},{4,8},{8,12},{12,16},{16,20},{20,24},{24,28},{28,0},{1,5},{5... | collective-permute-start | bytes 1935368 | tf_op jit(solution)/shard_map/ppermute | solution.py:246
  41.0 0.0 all-to-all-done.own0
  41.0 2.9 %collective-permute-start = (bf16[16,16,972]{2,1,0:T(8,128)(2,1)S(1)}, bf16[16,16,972]{2,1,0:T(8,128)(2,1)S(1)}, u32[]{:S(2)}, u32[]{:S(2)}) collective-permute-start(bf16[16,16,972]{2,1,0:T(8,128)(2,1)S(1)} %all-to-all-done.own0), channel_id=1, source_target_pairs={{0,1},{1,0},{2,3},{3,2},{4,5},{5,4},{6,7},{7,6},{8,9},{9,8},{10,11... | collective-permute-start | bytes 1493000 | tf_op jit(solution)/shard_map/ppermute | solution.py:246
  43.9 8.5 %collective-permute-done.6.refs_2_ = bf16[168,1920]{1,0:T(8,128)(2,1)} collective-permute-done((bf16[168,1920]{1,0:T(8,128)(2,1)S(1)}, bf16[168,1920]{1,0:T(8,128)(2,1)}, u32[]{:S(2)}, u32[]{:S(2)}) %collective-permute-start.6) | collective-permute-done | bytes 645152 | tf_op jit(solution)/shard_map/ppermute | solution.py:246
  52.4 5.7 %collective-permute-start.7 = (bf16[168,1920]{1,0:T(8,128)(2,1)}, bf16[168,1920]{1,0:T(8,128)(2,1)S(1)}, u32[]{:S(2)}, u32[]{:S(2)}) collective-permute-start(bf16[168,1920]{1,0:T(8,128)(2,1)} %collective-permute-done.6.refs_2_), channel_id=1, source_target_pairs={{0,28},{4,0},{8,4},{12,8},{16,12},{20,16},{24,20},{28,24},{1,29},{... | collective-permute-start | bytes 1935368 | tf_op jit(solution)/shard_map/ppermute | solution.py:246
  58.1 0.0 collective-permute-done.4.refs_1_
  58.1 1.9 %collective-permute-start.5 = (bf16[168,1920]{1,0:T(8,128)(2,1)}, bf16[168,1920]{1,0:T(8,128)(2,1)}, u32[]{:S(2)}, u32[]{:S(2)}) collective-permute-start(bf16[168,1920]{1,0:T(8,128)(2,1)} %collective-permute-done.4.refs_1_), channel_id=1, source_target_pairs={{0,4},{4,8},{8,12},{12,16},{16,20},{20,24},{24,28},{28,0},{1,5},{5... | collective-permute-start | bytes 1935368 | tf_op jit(solution)/shard_map/ppermute | solution.py:246
  60.0 1.9 %collective-permute-start.1 = (bf16[16,16,972]{2,1,0:T(8,128)(2,1)S(1)}, bf16[16,16,972]{2,1,0:T(8,128)(2,1)S(1)}, u32[]{:S(2)}, u32[]{:S(2)}) collective-permute-start(bf16[16,16,972]{2,1,0:T(8,128)(2,1)S(1)} %all-to-all-done.own0), channel_id=1, source_target_pairs={{0,2},{2,0},{1,3},{3,1},{4,6},{6,4},{5,7},{7,5},{8,10},{10,8},{9,1... | collective-permute-start | bytes 1493000 | tf_op jit(solution)/shard_map/ppermute | solution.py:246
  61.9 0.0 collective-permute-done.own1
  62.0 2.4 %collective-permute-start.2 = (bf16[16,16,972]{2,1,0:T(8,128)(2,1)S(1)}, bf16[16,16,972]{2,1,0:T(8,128)(2,1)S(1)}, u32[]{:S(2)}, u32[]{:S(2)}) collective-permute-start(bf16[16,16,972]{2,1,0:T(8,128)(2,1)S(1)} %collective-permute-done.own1), channel_id=1, source_target_pairs={{0,2},{2,0},{1,3},{3,1},{4,6},{6,4},{5,7},{7,5},{8,10},{10,8},{9,1... | collective-permute-start | bytes 1493000 | tf_op jit(solution)/shard_map/ppermute | solution.py:246
  64.4 0.0 collective-permute-done.1.oth0
  64.4 1.5 collective-permute-done.2.oth1
  65.9 3.4 %shard_map.50.refs_2_ = bf16[16,2,16,486]{3,2,1,0:T(8,128)(2,1)S(1)} custom-call(s32[1]{0:T(128)} %bitcast.4.core_ref, bf16[16,16,972]{2,1,0:T(8,128)(2,1)S(1)} %all-to-all-done.own0, bf16[16,16,972]{2,1,0:T(8,128)(2,1)S(1)} %collective-permute-done.own1, bf16[16,16,972]{2,1,0:T(8,128)(2,1)S(1)} %collective-permute-done.1.oth0, ...), custom_call_target="tpu_custom_call" | custom-call | flops 967458816 | bytes 4377888 | tf_op jit(solution)/shard_map/pallas_call | solution.py:120
  69.3 1.6 collective-permute-done.7.refs_1_
  70.9 0.0 copy-start.2
  70.9 5.3 %collective-permute-done.5.refs_0_ = bf16[168,1920]{1,0:T(8,128)(2,1)} collective-permute-done((bf16[168,1920]{1,0:T(8,128)(2,1)}, bf16[168,1920]{1,0:T(8,128)(2,1)}, u32[]{:S(2)}, u32[]{:S(2)}) %collective-permute-start.5) | collective-permute-done | bytes 645152 | tf_op jit(solution)/shard_map/ppermute | solution.py:246
  76.2 2.7 %shard_map.51 = bf16[16,2,16,810]{3,2,1,0:T(8,128)(2,1)S(1)} custom-call(s32[1]{0:T(128)} %bitcast.4.core_ref, bf16[16,16,972]{2,1,0:T(8,128)(2,1)S(1)} %all-to-all-done.own0, bf16[16,16,972]{2,1,0:T(8,128)(2,1)S(1)} %collective-permute-done.own1, bf16[16,16,972]{2,1,0:T(8,128)(2,1)S(1)} %collective-permute-done.1.oth0, ...), custom_call_target="tpu_custom_call" | custom-call | flops 644972544 | bytes 4079808 | tf_op jit(solution)/shard_map/pallas_call | solution.py:120
  78.9 0.0 copy-done.2
  78.9 0.0 copy-start
  78.9 0.9 copy-done
  79.9 8.7 %all-to-all-start.1 = ((bf16[16,2,16,810]{3,2,1,0:T(8,128)(2,1)}), bf16[16,2,16,810]{3,2,1,0:T(8,128)(2,1)S(1)}, u32[]{:S(2)}, u32[]{:S(2)}) async-start(bf16[16,2,16,810]{3,2,1,0:T(8,128)(2,1)} %copy-done), calls=%async_computation.1 | async-start | bytes 1835008 | tf_op jit(solution)/shard_map/all_to_all | solution.py:299
  88.6 1.9 %collective-permute-start.9 = (bf16[168,1920]{1,0:T(8,128)(2,1)}, bf16[168,1920]{1,0:T(8,128)(2,1)S(1)}, u32[]{:S(2)}, u32[]{:S(2)}) collective-permute-start(bf16[168,1920]{1,0:T(8,128)(2,1)} %collective-permute-done.5.refs_0_), channel_id=1, source_target_pairs={{0,4},{4,8},{8,12},{12,16},{16,20},{20,24},{24,28},{28,0},{1,5},{5... | collective-permute-start | bytes 1935368 | tf_op jit(solution)/shard_map/ppermute | solution.py:246
  90.5 5.1 %collective-permute-start.11 = (bf16[168,1920]{1,0:T(8,128)(2,1)}, bf16[168,1920]{1,0:T(8,128)(2,1)S(1)}, u32[]{:S(2)}, u32[]{:S(2)}) collective-permute-start(bf16[168,1920]{1,0:T(8,128)(2,1)} %copy-done.2), channel_id=1, source_target_pairs={{0,28},{4,0},{8,4},{12,8},{16,12},{20,16},{24,20},{28,24},{1,29},{... | collective-permute-start | bytes 1935368 | tf_op jit(solution)/shard_map/ppermute | solution.py:246
  95.6 9.5 %collective-permute-done.9.refs_0_ = bf16[168,1920]{1,0:T(8,128)(2,1)S(1)} collective-permute-done((bf16[168,1920]{1,0:T(8,128)(2,1)}, bf16[168,1920]{1,0:T(8,128)(2,1)S(1)}, u32[]{:S(2)}, u32[]{:S(2)}) %collective-permute-start.9) | collective-permute-done | bytes 645152 | tf_op jit(solution)/shard_map/ppermute | solution.py:246
  105.2 1.9 %collective-permute-start.10 = (bf16[168,1920]{1,0:T(8,128)(2,1)S(1)}, bf16[168,1920]{1,0:T(8,128)(2,1)S(1)}, u32[]{:S(2)}, u32[]{:S(2)}) collective-permute-start(bf16[168,1920]{1,0:T(8,128)(2,1)S(1)} %collective-permute-done.9.refs_0_), channel_id=1, source_target_pairs={{0,4},{4,8},{8,12},{12,16},{16,20},{20,24},{24,28},{28,0},{1,5},{5... | collective-permute-start | bytes 1935368 | tf_op jit(solution)/shard_map/ppermute | solution.py:246
  107.1 0.0 collective-permute-done.11.refs_1_
  107.1 1.6 shard_map.54.refs_1_
  108.7 12.0 %collective-permute-done.10.refs_0_ = bf16[168,1920]{1,0:T(8,128)(2,1)S(1)} collective-permute-done((bf16[168,1920]{1,0:T(8,128)(2,1)S(1)}, bf16[168,1920]{1,0:T(8,128)(2,1)S(1)}, u32[]{:S(2)}, u32[]{:S(2)}) %collective-permute-start.10) | collective-permute-done | bytes 645152 | tf_op jit(solution)/shard_map/ppermute | solution.py:246
  120.7 1.8 %shard_map.55 = bf16[16,2,16,486]{3,2,1,0:T(8,128)(2,1)} custom-call(s32[1]{0:T(128)} %bitcast.4.core_ref, bf16[16,16,972]{2,1,0:T(8,128)(2,1)S(1)} %all-to-all-done.own0, bf16[16,16,972]{2,1,0:T(8,128)(2,1)S(1)} %collective-permute-done.own1, bf16[16,16,972]{2,1,0:T(8,128)(2,1)S(1)} %collective-permute-done.1.oth0, ...), custom_call_target="tpu_custom_call" | custom-call | flops 322486272 | bytes 3118176 | tf_op jit(solution)/shard_map/pallas_call | solution.py:120
  122.5 0.0 all-to-all-done.1.x_ref
  122.5 9.8 %all-to-all-start.2 = ((bf16[32,16,486]{2,1,0:T(8,128)(2,1)}), bf16[32,16,486]{2,1,0:T(8,128)(2,1)S(1)}, u32[]{:S(2)}, u32[]{:S(2)}) async-start(bf16[32,16,486]{2,1,0:T(8,128)(2,1)} %bitcast.7), calls=%async_computation.2 | async-start | bytes 1048576 | tf_op jit(solution)/shard_map/all_to_all | solution.py:319
  132.3 0.2 shard_map.52
  132.5 2.0 %collective-permute-start.8 = (bf16[5,16,162]{2,1,0:T(8,128)(2,1)S(1)}, bf16[5,16,162]{2,1,0:T(8,128)(2,1)S(1)}, u32[]{:S(2)}, u32[]{:S(2)}) collective-permute-start(bf16[5,16,162]{2,1,0:T(8,128)(2,1)S(1)} %get-tuple-element.12), channel_id=1, source_target_pairs={{0,2},{2,0},{1,3},{3,1},{4,6},{6,4},{5,7},{7,5},{8,10},{10,8},{9,1... | collective-permute-start | bytes 77768 | tf_op jit(solution)/shard_map/ppermute | solution.py:246
  134.6 1.1 collective-permute-done.8.oth_ref
  135.6 0.1 shard_map.53.refs_0_
  135.7 1.9 %collective-permute-start.12 = (bf16[5,16,324]{2,1,0:T(8,128)(2,1)S(1)}, bf16[5,16,324]{2,1,0:T(8,128)(2,1)S(1)}, u32[]{:S(2)}, u32[]{:S(2)}) collective-permute-start(bf16[5,16,324]{2,1,0:T(8,128)(2,1)S(1)} %shard_map.53.refs_0_), channel_id=1, source_target_pairs={{0,0},{1,1},{2,32},{3,33},{4,64},{5,65},{6,96},{7,97},{8,128},{9,1... | collective-permute-start | bytes 155528 | tf_op jit(solution)/shard_map/ppermute | solution.py:331
  137.7 11.5 %all-to-all-done.2 = bf16[32,16,486]{2,1,0:T(8,128)(2,1)S(1)} async-done(((bf16[32,16,486]{2,1,0:T(8,128)(2,1)}), bf16[32,16,486]{2,1,0:T(8,128)(2,1)S(1)}, u32[]{:S(2)}, u32[]{:S(2)}) %all-to-all-start.2) | async-done | bytes 497696 | tf_op jit(solution)/shard_map/all_to_all | solution.py:319
  149.1 0.1 shard_map.56.refs_1_
  149.3 1.9 %collective-permute-start.13 = (bf16[3,16,324]{2,1,0:T(8,128)(2,1)S(1)}, bf16[3,16,324]{2,1,0:T(8,128)(2,1)S(1)}, u32[]{:S(2)}, u32[]{:S(2)}) collective-permute-start(bf16[3,16,324]{2,1,0:T(8,128)(2,1)S(1)} %shard_map.56.refs_1_), channel_id=1, source_target_pairs={{0,0},{1,1},{2,32},{3,33},{4,64},{5,65},{6,96},{7,97},{8,128},{9,1... | collective-permute-start | bytes 93320 | tf_op jit(solution)/shard_map/ppermute | solution.py:331
  151.2 0.0 copy-start.4
  151.2 0.0 copy-start.5
  151.2 0.6 copy-done.4
  151.9 0.0 copy-done.5
  151.9 0.6 shard_map.46.mask_ref
  152.4 0.0 collective-permute-done.12.refs_2_
  152.5 11.4 %collective-permute-done.13.refs_3_ = bf16[3,16,324]{2,1,0:T(8,128)(2,1)S(1)} collective-permute-done((bf16[3,16,324]{2,1,0:T(8,128)(2,1)S(1)}, bf16[3,16,324]{2,1,0:T(8,128)(2,1)S(1)}, u32[]{:S(2)}, u32[]{:S(2)}) %collective-permute-start.13) | collective-permute-done | bytes 31136 | tf_op jit(solution)/shard_map/ppermute | solution.py:331
  163.9 0.2 shard_map.57.own_ref
  164.0 2.0 %collective-permute-start.14 = (bf16[8,16,324]{2,1,0:T(8,128)(2,1)S(1)}, bf16[8,16,324]{2,1,0:T(8,128)(2,1)S(1)}, u32[]{:S(2)}, u32[]{:S(2)}) collective-permute-start(bf16[8,16,324]{2,1,0:T(8,128)(2,1)S(1)} %shard_map.57.own_ref), channel_id=1, source_target_pairs={{0,1},{1,0},{2,3},{3,2},{4,5},{5,4},{6,7},{7,6},{8,9},{9,8},{10,11... | collective-permute-start | bytes 248840 | tf_op jit(solution)/shard_map/ppermute | solution.py:246
  166.1 4.5 %collective-permute-done.14.oth_ref = bf16[8,16,324]{2,1,0:T(8,128)(2,1)S(1)} collective-permute-done((bf16[8,16,324]{2,1,0:T(8,128)(2,1)S(1)}, bf16[8,16,324]{2,1,0:T(8,128)(2,1)S(1)}, u32[]{:S(2)}, u32[]{:S(2)}) %collective-permute-start.14) | collective-permute-done | bytes 82976 | tf_op jit(solution)/shard_map/ppermute | solution.py:246
  170.6 1.0 shard_map.58
Async XLA Ops:
  0.0 1.0 copy-start.3
  2.6 9.7 %copy-start.1 = (bf16[324,3,324]{2,0,1:T(8,128)(2,1)S(1)}, bf16[324,3,324]{2,0,1:T(8,128)(2,1)}, u32[]{:S(2)}) copy-start(bf16[324,3,324]{2,0,1:T(8,128)(2,1)} %param.5) | copy-start | bytes 1889572
  2.6 38.4 %all-to-all-start = ((bf16[16,16,972]{2,1,0:T(8,128)(2,1)}), bf16[16,16,972]{2,1,0:T(8,128)(2,1)S(1)}, u32[]{:S(2)}, u32[]{:S(2)}) async-start(bf16[16,16,972]{2,1,0:T(8,128)(2,1)} %shard_map.47), calls=%async_computation | async-start | bytes 1048576 | tf_op jit(solution)/shard_map/all_to_all | solution.py:279
  12.5 15.4 %collective-permute-start.3 = (bf16[168,972]{1,0:T(8,128)(2,1)S(1)}, bf16[168,972]{1,0:T(8,128)(2,1)S(1)}, u32[]{:S(2)}, u32[]{:S(2)}) collective-permute-start(bf16[168,972]{1,0:T(8,128)(2,1)S(1)} %get-tuple-element.10), channel_id=1, source_target_pairs={{0,1},{1,0},{2,3},{3,2},{4,5},{5,4},{6,7},{7,6},{8,9},{9,8},{10,11... | collective-permute-start | bytes 979784 | tf_op jit(solution)/shard_map/ppermute | solution.py:246
  28.1 24.3 %collective-permute-start.6 = (bf16[168,1920]{1,0:T(8,128)(2,1)S(1)}, bf16[168,1920]{1,0:T(8,128)(2,1)}, u32[]{:S(2)}, u32[]{:S(2)}) collective-permute-start(bf16[168,1920]{1,0:T(8,128)(2,1)S(1)} %shard_map.49.refs_0_), channel_id=1, source_target_pairs={{0,28},{4,0},{8,4},{12,8},{16,12},{20,16},{24,20},{28,24},{1,29},{... | collective-permute-start | bytes 1935368 | tf_op jit(solution)/shard_map/ppermute | solution.py:246
  39.0 19.0 %collective-permute-start.4 = (bf16[168,1920]{1,0:T(8,128)(2,1)S(1)}, bf16[168,1920]{1,0:T(8,128)(2,1)}, u32[]{:S(2)}, u32[]{:S(2)}) collective-permute-start(bf16[168,1920]{1,0:T(8,128)(2,1)S(1)} %shard_map.49.refs_0_), channel_id=1, source_target_pairs={{0,4},{4,8},{8,12},{12,16},{16,20},{20,24},{24,28},{28,0},{1,5},{5... | collective-permute-start | bytes 1935368 | tf_op jit(solution)/shard_map/ppermute | solution.py:246
  41.0 21.0 %collective-permute-start = (bf16[16,16,972]{2,1,0:T(8,128)(2,1)S(1)}, bf16[16,16,972]{2,1,0:T(8,128)(2,1)S(1)}, u32[]{:S(2)}, u32[]{:S(2)}) collective-permute-start(bf16[16,16,972]{2,1,0:T(8,128)(2,1)S(1)} %all-to-all-done.own0), channel_id=1, source_target_pairs={{0,1},{1,0},{2,3},{3,2},{4,5},{5,4},{6,7},{7,6},{8,9},{9,8},{10,11... | collective-permute-start | bytes 1493000 | tf_op jit(solution)/shard_map/ppermute | solution.py:246
  52.4 18.5 %collective-permute-start.7 = (bf16[168,1920]{1,0:T(8,128)(2,1)}, bf16[168,1920]{1,0:T(8,128)(2,1)S(1)}, u32[]{:S(2)}, u32[]{:S(2)}) collective-permute-start(bf16[168,1920]{1,0:T(8,128)(2,1)} %collective-permute-done.6.refs_2_), channel_id=1, source_target_pairs={{0,28},{4,0},{8,4},{12,8},{16,12},{20,16},{24,20},{28,24},{1,29},{... | collective-permute-start | bytes 1935368 | tf_op jit(solution)/shard_map/ppermute | solution.py:246
  58.1 18.1 %collective-permute-start.5 = (bf16[168,1920]{1,0:T(8,128)(2,1)}, bf16[168,1920]{1,0:T(8,128)(2,1)}, u32[]{:S(2)}, u32[]{:S(2)}) collective-permute-start(bf16[168,1920]{1,0:T(8,128)(2,1)} %collective-permute-done.4.refs_1_), channel_id=1, source_target_pairs={{0,4},{4,8},{8,12},{12,16},{16,20},{20,24},{24,28},{28,0},{1,5},{5... | collective-permute-start | bytes 1935368 | tf_op jit(solution)/shard_map/ppermute | solution.py:246
  60.0 4.4 %collective-permute-start.1 = (bf16[16,16,972]{2,1,0:T(8,128)(2,1)S(1)}, bf16[16,16,972]{2,1,0:T(8,128)(2,1)S(1)}, u32[]{:S(2)}, u32[]{:S(2)}) collective-permute-start(bf16[16,16,972]{2,1,0:T(8,128)(2,1)S(1)} %all-to-all-done.own0), channel_id=1, source_target_pairs={{0,2},{2,0},{1,3},{3,1},{4,6},{6,4},{5,7},{7,5},{8,10},{10,8},{9,1... | collective-permute-start | bytes 1493000 | tf_op jit(solution)/shard_map/ppermute | solution.py:246
  62.0 3.9 %collective-permute-start.2 = (bf16[16,16,972]{2,1,0:T(8,128)(2,1)S(1)}, bf16[16,16,972]{2,1,0:T(8,128)(2,1)S(1)}, u32[]{:S(2)}, u32[]{:S(2)}) collective-permute-start(bf16[16,16,972]{2,1,0:T(8,128)(2,1)S(1)} %collective-permute-done.own1), channel_id=1, source_target_pairs={{0,2},{2,0},{1,3},{3,1},{4,6},{6,4},{5,7},{7,5},{8,10},{10,8},{9,1... | collective-permute-start | bytes 1493000 | tf_op jit(solution)/shard_map/ppermute | solution.py:246
  70.9 8.0 %copy-start.2 = (bf16[168,1920]{1,0:T(8,128)(2,1)}, bf16[168,1920]{1,0:T(8,128)(2,1)S(1)}, u32[]{:S(2)}) copy-start(bf16[168,1920]{1,0:T(8,128)(2,1)S(1)} %collective-permute-done.7.refs_1_) | copy-start | bytes 1935364
  78.9 1.0 copy-start
  79.9 42.6 %all-to-all-start.1 = ((bf16[16,2,16,810]{3,2,1,0:T(8,128)(2,1)}), bf16[16,2,16,810]{3,2,1,0:T(8,128)(2,1)S(1)}, u32[]{:S(2)}, u32[]{:S(2)}) async-start(bf16[16,2,16,810]{3,2,1,0:T(8,128)(2,1)} %copy-done), calls=%async_computation.1 | async-start | bytes 1835008 | tf_op jit(solution)/shard_map/all_to_all | solution.py:299
  88.6 16.6 %collective-permute-start.9 = (bf16[168,1920]{1,0:T(8,128)(2,1)}, bf16[168,1920]{1,0:T(8,128)(2,1)S(1)}, u32[]{:S(2)}, u32[]{:S(2)}) collective-permute-start(bf16[168,1920]{1,0:T(8,128)(2,1)} %collective-permute-done.5.refs_0_), channel_id=1, source_target_pairs={{0,4},{4,8},{8,12},{12,16},{16,20},{20,24},{24,28},{28,0},{1,5},{5... | collective-permute-start | bytes 1935368 | tf_op jit(solution)/shard_map/ppermute | solution.py:246
  90.5 16.6 %collective-permute-start.11 = (bf16[168,1920]{1,0:T(8,128)(2,1)}, bf16[168,1920]{1,0:T(8,128)(2,1)S(1)}, u32[]{:S(2)}, u32[]{:S(2)}) collective-permute-start(bf16[168,1920]{1,0:T(8,128)(2,1)} %copy-done.2), channel_id=1, source_target_pairs={{0,28},{4,0},{8,4},{12,8},{16,12},{20,16},{24,20},{28,24},{1,29},{... | collective-permute-start | bytes 1935368 | tf_op jit(solution)/shard_map/ppermute | solution.py:246
  105.2 15.5 %collective-permute-start.10 = (bf16[168,1920]{1,0:T(8,128)(2,1)S(1)}, bf16[168,1920]{1,0:T(8,128)(2,1)S(1)}, u32[]{:S(2)}, u32[]{:S(2)}) collective-permute-start(bf16[168,1920]{1,0:T(8,128)(2,1)S(1)} %collective-permute-done.9.refs_0_), channel_id=1, source_target_pairs={{0,4},{4,8},{8,12},{12,16},{16,20},{20,24},{24,28},{28,0},{1,5},{5... | collective-permute-start | bytes 1935368 | tf_op jit(solution)/shard_map/ppermute | solution.py:246
  122.5 26.6 %all-to-all-start.2 = ((bf16[32,16,486]{2,1,0:T(8,128)(2,1)}), bf16[32,16,486]{2,1,0:T(8,128)(2,1)S(1)}, u32[]{:S(2)}, u32[]{:S(2)}) async-start(bf16[32,16,486]{2,1,0:T(8,128)(2,1)} %bitcast.7), calls=%async_computation.2 | async-start | bytes 1048576 | tf_op jit(solution)/shard_map/all_to_all | solution.py:319
  132.5 3.1 %collective-permute-start.8 = (bf16[5,16,162]{2,1,0:T(8,128)(2,1)S(1)}, bf16[5,16,162]{2,1,0:T(8,128)(2,1)S(1)}, u32[]{:S(2)}, u32[]{:S(2)}) collective-permute-start(bf16[5,16,162]{2,1,0:T(8,128)(2,1)S(1)} %get-tuple-element.12), channel_id=1, source_target_pairs={{0,2},{2,0},{1,3},{3,1},{4,6},{6,4},{5,7},{7,5},{8,10},{10,8},{9,1... | collective-permute-start | bytes 77768 | tf_op jit(solution)/shard_map/ppermute | solution.py:246
  135.7 16.7 %collective-permute-start.12 = (bf16[5,16,324]{2,1,0:T(8,128)(2,1)S(1)}, bf16[5,16,324]{2,1,0:T(8,128)(2,1)S(1)}, u32[]{:S(2)}, u32[]{:S(2)}) collective-permute-start(bf16[5,16,324]{2,1,0:T(8,128)(2,1)S(1)} %shard_map.53.refs_0_), channel_id=1, source_target_pairs={{0,0},{1,1},{2,32},{3,33},{4,64},{5,65},{6,96},{7,97},{8,128},{9,1... | collective-permute-start | bytes 155528 | tf_op jit(solution)/shard_map/ppermute | solution.py:331
  149.3 14.6 %collective-permute-start.13 = (bf16[3,16,324]{2,1,0:T(8,128)(2,1)S(1)}, bf16[3,16,324]{2,1,0:T(8,128)(2,1)S(1)}, u32[]{:S(2)}, u32[]{:S(2)}) collective-permute-start(bf16[3,16,324]{2,1,0:T(8,128)(2,1)S(1)} %shard_map.56.refs_1_), channel_id=1, source_target_pairs={{0,0},{1,1},{2,32},{3,33},{4,64},{5,65},{6,96},{7,97},{8,128},{9,1... | collective-permute-start | bytes 93320 | tf_op jit(solution)/shard_map/ppermute | solution.py:331
  151.2 0.7 copy-start.4
  151.2 0.7 copy-start.5
  164.0 6.5 %collective-permute-start.14 = (bf16[8,16,324]{2,1,0:T(8,128)(2,1)S(1)}, bf16[8,16,324]{2,1,0:T(8,128)(2,1)S(1)}, u32[]{:S(2)}, u32[]{:S(2)}) collective-permute-start(bf16[8,16,324]{2,1,0:T(8,128)(2,1)S(1)} %shard_map.57.own_ref), channel_id=1, source_target_pairs={{0,1},{1,0},{2,3},{3,2},{4,5},{5,4},{6,7},{7,6},{8,9},{9,8},{10,11... | collective-permute-start | bytes 248840 | tf_op jit(solution)/shard_map/ppermute | solution.py:246
